TPU v7x, 32 devices: a whole 2x2x4 slice. The times are simulated.
32 devices in a mesh: group: 8 (over y, x, core), rep: 4 (over z).
Axes of the slice: x: 2, y: 2, z: 4, core: 2. Of those that a mesh axis runs over, the one named last changes fastest.
Arguments:
- tokens: bfloat16 [8192, 768], P(('group', 'rep')), may hold values from -6 to 6
- segments: int32 [8192], P(('group', 'rep')), may hold values from -1 to 3, as said below
- attn_in_weight: bfloat16 [2, 768, 2304], P(None, 'group'), may hold values from -8 to 8
- attn_bias: bfloat16 [2, 3, 768], P(None, None, 'group'), may hold values from -1.75 to 1.75
- out_weight: bfloat16 [2, 768, 768], P(None, 'group'), may hold values from -0.875 to 0.875
- fc1_weight: bfloat16 [2, 768, 3072], P(None, 'group'), may hold values from -0.21875 to 0.21875
- fc1_bias: bfloat16 [2, 3072], P(None, 'group'), may hold values from -1.75 to 1.75
- fc2_weight: bfloat16 [2, 3072, 768], P(None, 'group'), may hold values from -0.109375 to 0.109375
- fc2_bias: bfloat16 [2, 768], P(None, 'group'), may hold values from -1.75 to 1.75
- ln_gain: bfloat16 [2, 2, 768], P(None, None, 'group'), may hold values from 0.25 to 1.75
- ln_bias: bfloat16 [2, 2, 768], P(None, None, 'group'), may hold values from -1.75 to 1.75
- cotangent: bfloat16 [8192, 768], P(('group', 'rep')), may hold values from -12 to 12
Outputs:
- output: float32 [8192, 768], P(('group', 'rep'))
- input_grad: float32 [8192, 768], P(('group', 'rep'))
- grad_attn_in: float32 [2, 768, 2304], P(None, 'group')
- grad_attn_bias: float32 [2, 3, 768], P(None, None, 'group')
- grad_out_weight: float32 [2, 768, 768], P(None, 'group')
- grad_fc1_weight: float32 [2, 768, 3072], P(None, 'group')
- grad_fc1_bias: float32 [2, 3072], P(None, 'group')
- grad_fc2_weight: float32 [2, 3072, 768], P(None, 'group')
- grad_fc2_bias: float32 [2, 768], P(None, 'group')
- grad_ln_gain: float32 [2, 2, 768], P(None, None, 'group')
- grad_ln_bias: float32 [2, 2, 768], P(None, None, 'group')
Inputs may be any that keep to these rules, and one draw needn't show every extreme that they name: `segments`: each clip occupies exactly 1500 consecutive positions, clip numbers rise by one along the tokens, the first clip starts at the first token, padding elsewhere.
All inputs are finite; a program needn't handle non-finite values.
Results may differ from a plain program's by a relative error of at most 0.017.
Values may be sent and summed in bfloat16 or wider, within the bound.
No kernel may reach another device: no remote copies, remote signals or barrier semaphores. Data moves between devices by JAX's collectives and lax.ppermute only.
A program may use at most 256 MiB of HBM per device.

v0:
```python
import jax
import jax.numpy as jnp
from jax import lax
from jax.sharding import PartitionSpec as P

H = 12
HD = 64
LAYERS = 2
REACH = 6
EPSILON = 1e-05


def passed_along(value, axis, steps):
    count = lax.axis_size(axis)
    leading, last = (max(0, -steps), min(count, count - steps))
    return lax.ppermute(value, axis, [(source, source + steps) for source in range(leading, last)])


def layer_norm(values, gain, offset):
    center = jnp.mean(values, axis=-1, keepdims=True)
    shifted = values - center
    spread = jnp.mean(shifted * shifted, axis=-1, keepdims=True)
    inverse = lax.rsqrt(spread + EPSILON)
    unit_rows = shifted * inverse
    return (unit_rows * gain.astype(jnp.float32) + offset.astype(jnp.float32), unit_rows, inverse)


def norm_back(upstream, unit_rows, inverse, gain):
    scaled = upstream * gain.astype(jnp.float32)
    result = inverse * (
        scaled
        - jnp.mean(scaled, axis=-1, keepdims=True)
        - unit_rows * jnp.mean(scaled * unit_rows, axis=-1, keepdims=True)
    )
    return (result, jnp.sum(upstream * unit_rows, axis=0), jnp.sum(upstream, axis=0))


def gelu_slope(inputs):
    normal_cdf = 0.5 * (1.0 + lax.erf(inputs * 0.7071067811865476))
    return normal_cdf + inputs * jnp.exp(-0.5 * inputs * inputs) * 0.3989422804014327


def split_heads(matrix):
    return matrix.reshape(matrix.shape[0], H // 2, 2, HD).transpose(1, 0, 2, 3)


def join_heads(stacked):
    return stacked.transpose(1, 0, 2, 3).reshape(stacked.shape[1], H * HD)


def head_forward(queries, key_block, value_block, allowed):
    scores = jnp.einsum("qhd,khd->hqk", queries, key_block, preferred_element_type=jnp.float32)
    scores = jnp.where(allowed[None], scores, -1e30)
    top_score = jnp.max(scores, axis=2, keepdims=True)
    expd = jnp.exp(scores - top_score)
    total = jnp.sum(expd, axis=2, keepdims=True)
    probs = (expd / total).astype(jnp.bfloat16)
    heard = jnp.einsum("hqk,khd->qhd", probs, value_block, preferred_element_type=jnp.float32)
    return (heard, top_score[:, :, 0] + jnp.log(total[:, :, 0]))


def head_backward(queries, key_block, value_block, allowed, log_totals, upstream):
    scores = jnp.einsum("qhd,khd->hqk", queries, key_block, preferred_element_type=jnp.float32)
    probs = jnp.where(allowed[None], jnp.exp(scores - log_totals[:, :, None]), 0.0)
    rounded = probs.astype(jnp.bfloat16)
    d_value = jnp.einsum("hqk,qhd->khd", rounded, upstream, preferred_element_type=jnp.float32)
    d_probs = jnp.einsum("qhd,khd->hqk", upstream, value_block, preferred_element_type=jnp.float32)
    delta = jnp.sum(probs * d_probs, axis=2, keepdims=True)
    d_scores = (probs * (d_probs - delta)).astype(jnp.bfloat16)
    d_query = jnp.einsum("hqk,khd->qhd", d_scores, key_block, preferred_element_type=jnp.float32)
    d_key = jnp.einsum("hqk,qhd->khd", d_scores, queries, preferred_element_type=jnp.float32)
    return (d_query, d_key, d_value)


def local(
    tokens,
    segments,
    attn_in_weight,
    attn_bias,
    out_weight,
    fc1_weight,
    fc1_bias,
    fc2_weight,
    fc2_bias,
    ln_gain,
    ln_bias,
    cotangent,
):
    tok_rows = tokens.shape[0]
    width = H * HD
    score_scale = HD ** (-0.5)
    labels = segments + 2
    own_place = lax.iota(jnp.int32, tok_rows) + REACH * tok_rows
    window_place = lax.iota(jnp.int32, (2 * REACH + 1) * tok_rows)
    resid = tokens.astype(jnp.float32)
    fetched = []
    every_store = []
    for layer_at in range(LAYERS):
        weights = (
            lax.all_gather(attn_in_weight[layer_at], "group", axis=0, tiled=True),
            lax.all_gather(attn_bias[layer_at], "group", axis=1, tiled=True),
            lax.all_gather(out_weight[layer_at], "group", axis=0, tiled=True),
            lax.all_gather(fc1_weight[layer_at], "group", axis=0, tiled=True),
            lax.all_gather(fc1_bias[layer_at], "group", axis=0, tiled=True),
            lax.all_gather(fc2_weight[layer_at], "group", axis=0, tiled=True),
            lax.all_gather(fc2_bias[layer_at], "group", axis=0, tiled=True),
            lax.all_gather(ln_gain[layer_at], "group", axis=1, tiled=True),
            lax.all_gather(ln_bias[layer_at], "group", axis=1, tiled=True),
        )
        (
            forward_w_in,
            forward_b_attn,
            forward_w_out,
            forward_w_up,
            forward_b_up,
            forward_w_down,
            forward_b_down,
            forward_gains,
            forward_offsets,
        ) = weights
        normed, forward_unit_first, forward_inverse_first = layer_norm(
            resid, forward_gains[0], forward_offsets[0]
        )
        forward_first = normed.astype(jnp.bfloat16)
        mixed = jnp.dot(forward_first, forward_w_in, preferred_element_type=jnp.float32)
        forward_queries = (
            (mixed[:, :width] + forward_b_attn[0].astype(jnp.float32)) * score_scale
        ).astype(jnp.bfloat16)
        forward_key_value = jnp.concatenate(
            [
                mixed[:, width : 2 * width],
                mixed[:, 2 * width :] + forward_b_attn[1].astype(jnp.float32),
            ],
            axis=1,
        ).astype(jnp.bfloat16)
        lower_parts = []
        upper_parts = []
        for gather_distance in range(1, REACH + 1):
            lower_parts.append(
                passed_along((forward_key_value, labels), ("group", "rep"), gather_distance)
            )
            upper_parts.append(
                passed_along((forward_key_value, labels), ("group", "rep"), -gather_distance)
            )
        ordered = lower_parts[::-1] + [(forward_key_value, labels)] + upper_parts
        window_rows = jnp.concatenate([member[0] for member in ordered], axis=0)
        window_labels = jnp.concatenate([member[1] for member in ordered], axis=0)
        same = labels[:, None] == window_labels[None, :]
        forward_allowed = same & (
            (labels[:, None] >= 2) | (own_place[:, None] == window_place[None, :])
        )

        def attend_pair(members):
            return head_forward(members[0], members[1], members[2], forward_allowed)

        attended, forward_log_totals = lax.map(
            attend_pair,
            (
                split_heads(forward_queries),
                split_heads(window_rows[:, :width]),
                split_heads(window_rows[:, width:]),
            ),
        )
        forward_heard = join_heads(attended).astype(jnp.bfloat16)
        middle = (
            resid
            + jnp.dot(forward_heard, forward_w_out, preferred_element_type=jnp.float32)
            + forward_b_attn[2].astype(jnp.float32)
        )
        normed_two, forward_unit_second, forward_inverse_second = layer_norm(
            middle, forward_gains[1], forward_offsets[1]
        )
        forward_second = normed_two.astype(jnp.bfloat16)
        forward_pre_act = jnp.dot(
            forward_second, forward_w_up, preferred_element_type=jnp.float32
        ) + forward_b_up.astype(jnp.float32)
        forward_active = jax.nn.gelu(forward_pre_act, approximate=False).astype(jnp.bfloat16)
        result = (
            middle
            + jnp.dot(forward_active, forward_w_down, preferred_element_type=jnp.float32)
            + forward_b_down.astype(jnp.float32)
        )
        forward_stored = (
            forward_unit_first,
            forward_inverse_first,
            forward_first,
            forward_queries,
            window_rows,
            forward_allowed,
            forward_heard,
            forward_log_totals,
            forward_unit_second,
            forward_inverse_second,
            forward_second,
            forward_pre_act,
            forward_active,
        )
        resid = result
        fetched.append(None)
        every_store.append(forward_stored)
    upstream = cotangent.astype(jnp.float32)
    shares = [None] * LAYERS
    for layer_at in reversed(range(LAYERS)):
        weights = (
            lax.all_gather(attn_in_weight[layer_at], "group", axis=0, tiled=True),
            lax.all_gather(attn_bias[layer_at], "group", axis=1, tiled=True),
            lax.all_gather(out_weight[layer_at], "group", axis=0, tiled=True),
            lax.all_gather(fc1_weight[layer_at], "group", axis=0, tiled=True),
            lax.all_gather(fc1_bias[layer_at], "group", axis=0, tiled=True),
            lax.all_gather(fc2_weight[layer_at], "group", axis=0, tiled=True),
            lax.all_gather(fc2_bias[layer_at], "group", axis=0, tiled=True),
            lax.all_gather(ln_gain[layer_at], "group", axis=1, tiled=True),
            lax.all_gather(ln_bias[layer_at], "group", axis=1, tiled=True),
        )
        w_in, b_attn, w_out, w_up, b_up, w_down, b_down, gains, offsets = weights
        (
            unit_first,
            inverse_first,
            first,
            queries,
            window_kv,
            allowed,
            heard,
            log_totals,
            unit_second,
            inverse_second,
            second,
            pre_act,
            active,
        ) = every_store[layer_at]
        down_rounded = upstream.astype(jnp.bfloat16)
        g_down_b = jnp.sum(upstream, axis=0)
        g_down_w = jnp.einsum("tf,td->fd", active, down_rounded, preferred_element_type=jnp.float32)
        d_pre = jnp.einsum(
            "td,fd->tf", down_rounded, w_down, preferred_element_type=jnp.float32
        ) * gelu_slope(pre_act)
        up_rounded = d_pre.astype(jnp.bfloat16)
        g_up_b = jnp.sum(d_pre, axis=0)
        g_up_w = jnp.einsum("td,tf->df", second, up_rounded, preferred_element_type=jnp.float32)
        d_second = jnp.einsum("tf,df->td", up_rounded, w_up, preferred_element_type=jnp.float32)
        d_norm_two, g_gain_two, g_offset_two = norm_back(
            d_second, unit_second, inverse_second, gains[1]
        )
        d_middle = upstream + d_norm_two
        middle_rounded = d_middle.astype(jnp.bfloat16)
        g_out_b = jnp.sum(d_middle, axis=0)
        g_out_w = jnp.einsum("td,te->de", heard, middle_rounded, preferred_element_type=jnp.float32)
        d_heard = jnp.einsum(
            "te,de->td", middle_rounded, w_out, preferred_element_type=jnp.float32
        ).astype(jnp.bfloat16)

        def pair_backward(members):
            return head_backward(
                members[0], members[1], members[2], allowed, members[3], members[4]
            )

        d_query, d_key, d_value = lax.map(
            pair_backward,
            (
                split_heads(queries),
                split_heads(window_kv[:, :width]),
                split_heads(window_kv[:, width:]),
                log_totals,
                split_heads(d_heard),
            ),
        )
        d_window = jnp.concatenate([join_heads(d_key), join_heads(d_value)], axis=1)
        d_own = d_window[REACH * tok_rows : (REACH + 1) * tok_rows]
        for distance in range(1, REACH + 1):
            lower_block = d_window[
                (REACH - distance) * tok_rows : (REACH - distance + 1) * tok_rows
            ]
            upper_block = d_window[
                (REACH + distance) * tok_rows : (REACH + distance + 1) * tok_rows
            ]
            d_own = d_own + passed_along(
                lower_block.astype(jnp.bfloat16), ("group", "rep"), -distance
            ).astype(lower_block.dtype)
            d_own = d_own + passed_along(
                upper_block.astype(jnp.bfloat16), ("group", "rep"), distance
            ).astype(upper_block.dtype)
        d_queries = join_heads(d_query) * score_scale
        d_mixed = jnp.concatenate([d_queries, d_own], axis=1)
        mixed_rounded = d_mixed.astype(jnp.bfloat16)
        g_attn_b = jnp.stack(
            [jnp.sum(d_queries, axis=0), jnp.sum(d_own[:, width:], axis=0), g_out_b]
        )
        g_in_w = jnp.einsum("td,te->de", first, mixed_rounded, preferred_element_type=jnp.float32)
        d_first = jnp.einsum("te,de->td", mixed_rounded, w_in, preferred_element_type=jnp.float32)
        d_norm_one, g_gain_one, g_offset_one = norm_back(
            d_first, unit_first, inverse_first, gains[0]
        )
        d_resid = d_middle + d_norm_one
        grads = (
            g_in_w,
            g_attn_b,
            g_out_w,
            g_up_w,
            g_up_b,
            g_down_w,
            g_down_b,
            jnp.stack([g_gain_one, g_gain_two]),
            jnp.stack([g_offset_one, g_offset_two]),
        )
        upstream, grads = (d_resid, grads)
        summed = (
            lax.psum_scatter(
                grads[0].astype(jnp.bfloat16), "group", scatter_dimension=0, tiled=True
            ).astype(jnp.float32),
            lax.psum_scatter(
                grads[1].astype(jnp.bfloat16), "group", scatter_dimension=1, tiled=True
            ).astype(jnp.float32),
            lax.psum_scatter(
                grads[2].astype(jnp.bfloat16), "group", scatter_dimension=0, tiled=True
            ).astype(jnp.float32),
            lax.psum_scatter(
                grads[3].astype(jnp.bfloat16), "group", scatter_dimension=0, tiled=True
            ).astype(jnp.float32),
            lax.psum_scatter(
                grads[4].astype(jnp.bfloat16), "group", scatter_dimension=0, tiled=True
            ).astype(jnp.float32),
            lax.psum_scatter(
                grads[5].astype(jnp.bfloat16), "group", scatter_dimension=0, tiled=True
            ).astype(jnp.float32),
            lax.psum_scatter(
                grads[6].astype(jnp.bfloat16), "group", scatter_dimension=0, tiled=True
            ).astype(jnp.float32),
            lax.psum_scatter(
                grads[7].astype(jnp.bfloat16), "group", scatter_dimension=1, tiled=True
            ).astype(jnp.float32),
            lax.psum_scatter(
                grads[8].astype(jnp.bfloat16), "group", scatter_dimension=1, tiled=True
            ).astype(jnp.float32),
        )
        summed = (
            lax.psum(summed[0].astype(jnp.bfloat16), "rep").astype(jnp.float32),
            lax.psum(summed[1].astype(jnp.bfloat16), "rep").astype(jnp.float32),
            lax.psum(summed[2].astype(jnp.bfloat16), "rep").astype(jnp.float32),
            lax.psum(summed[3].astype(jnp.bfloat16), "rep").astype(jnp.float32),
            lax.psum(summed[4].astype(jnp.bfloat16), "rep").astype(jnp.float32),
            lax.psum(summed[5].astype(jnp.bfloat16), "rep").astype(jnp.float32),
            lax.psum(summed[6].astype(jnp.bfloat16), "rep").astype(jnp.float32),
            lax.psum(summed[7].astype(jnp.bfloat16), "rep").astype(jnp.float32),
            lax.psum(summed[8].astype(jnp.bfloat16), "rep").astype(jnp.float32),
        )
        shares[layer_at] = summed
    stacked = [
        jnp.stack([shares[layer_at][field] for layer_at in range(LAYERS)]) for field in range(9)
    ]
    return (
        resid,
        upstream,
        stacked[0],
        stacked[1],
        stacked[2],
        stacked[3],
        stacked[4],
        stacked[5],
        stacked[6],
        stacked[7],
        stacked[8],
    )


def solution(mesh):
    in_specs = (
        P(("group", "rep"), None),
        P(("group", "rep")),
        P(None, "group", None),
        P(None, None, "group"),
        P(None, "group", None),
        P(None, "group", None),
        P(None, "group"),
        P(None, "group", None),
        P(None, "group"),
        P(None, None, "group"),
        P(None, None, "group"),
        P(("group", "rep"), None),
    )
    out_specs = (
        P(("group", "rep"), None),
        P(("group", "rep"), None),
        P(None, "group", None),
        P(None, None, "group"),
        P(None, "group", None),
        P(None, "group", None),
        P(None, "group"),
        P(None, "group", None),
        P(None, "group"),
        P(None, None, "group"),
        P(None, None, "group"),
    )
    return jax.shard_map(local, mesh=mesh, in_specs=in_specs, out_specs=out_specs, check_vma=False)
```

profile of v0, /device:TPU:0, one launch (start us, length us, event | category | flops | bytes accessed | tf_op | source)
XLA Modules:
  0.0 2316.4 jit_solution(14734667101272722325)
XLA Ops:
  34.2 12.0 all-gather
  51.0 8.5 all-gather.1
  64.3 10.5 all-gather.3
  74.9 7.8 fusion.231
  82.7 8.5 all-gather.6
  91.9 9.2 all-gather.9
  105.8 11.3 all-gather.10
  121.9 9.2 all-gather.12
  131.1 7.8 fusion.224
  140.5 14.0 all-reduce
  166.4 10.5 collective-permute-start
  190.0 8.8 collective-permute-start.3
  198.8 30.9 %collective-permute-done.23 = s32[256]{0:T(256)S(1)} collective-permute-done((s32[256]{0:T(256)S(1)}, s32[256]{0:T(256)S(1)}, u32[]{:S(2)}, u32[]{:S(2)}) %collective-permute-start.23) | collective-permute-done | bytes 1056 | tf_op jit(solution)/shard_map/ppermute | solution.py:16
  229.7 8.7 collective-permute-start.4
  238.5 32.8 %collective-permute-start.5 = (bf16[256,1536]{1,0:T(8,128)(2,1)S(1)}, bf16[256,1536]{1,0:T(8,128)(2,1)S(1)}, u32[]{:S(2)}, u32[]{:S(2)}) collective-permute-start(bf16[256,1536]{1,0:T(8,128)(2,1)S(1)} %pad_maximum_fusion.4), channel_id=1, source_target_pairs={{0,1},{1,2},{2,3},{3,4},{4,5},{5,6},{6,7},{7,8},{8,9},{9,10},{10,1... | collective-permute-start | bytes 2359304 | tf_op jit(solution)/shard_map/ppermute | solution.py:16
  292.3 18.6 collective-permute-done.6
  313.2 66.3 %collective-permute-done.7 = bf16[256,1536]{1,0:T(8,128)(2,1)S(1)} collective-permute-done((bf16[256,1536]{1,0:T(8,128)(2,1)S(1)}, bf16[256,1536]{1,0:T(8,128)(2,1)S(1)}, u32[]{:S(2)}, u32[]{:S(2)}) %collective-permute-start.7) | collective-permute-done | bytes 786464 | tf_op jit(solution)/shard_map/ppermute | solution.py:16
  383.3 12.7 collective-permute-done.11
  396.9 8.5 fusion.258
  405.4 7.8 copy.58
  413.1 7.8 copy.60
  421.0 46.2 %while.56 = (s32[]{:T(128)}, bf16[6,256,2,64]{1,3,2,0:T(8,128)(2,1)S(1)}, f32[6,2,256]{2,1,0:T(2,128)S(1)}, bf16[6,3328,2,64]{1,3,2,0:T(8,128)(2,1)}, bf16[6,256...) while((s32[]{:T(128)}, ...), condition=%wide.region_5.6_spmd.clone, body=%wide.region_2.5_spmd.clone.sunk | while | flops 451542528 | bytes 24085872 | solution.py:156
  469.6 11.4 fusion.130
  489.2 17.5 collective-permute-start.24
  506.7 14.5 collective-permute-start.25
  529.0 50.0 %all-gather.15 = bf16[1,3072]{1,0:T(2,128)(2,1)S(1)} all-gather(bf16[1,384]{1,0:T(2,128)(2,1)S(1)} %get-tuple-element.563), channel_id=17, replica_groups=mesh['group'=8,'rep'=4] {'group'}, dimensions={1}, use_global_device_ids=true | all-gather | bytes 6912 | tf_op jit(solution)/shard_map/all_gather | solution.py:104
  601.5 13.5 collective-permute-done.29
  618.3 8.3 collective-permute-done.30
  628.8 84.9 %collective-permute-done.31 = bf16[256,1536]{1,0:T(8,128)(2,1)S(1)} collective-permute-done((bf16[256,1536]{1,0:T(8,128)(2,1)S(1)}, bf16[256,1536]{1,0:T(8,128)(2,1)S(1)}, u32[]{:S(2)}, u32[]{:S(2)}) %collective-permute-start.31) | collective-permute-done | bytes 786464 | tf_op jit(solution)/shard_map/ppermute | solution.py:16
  717.5 10.0 collective-permute-done.35
  728.4 8.4 fusion.257
  736.8 7.8 copy.64
  744.6 7.7 copy.66
  752.4 46.2 %while.57 = (s32[]{:T(128)}, bf16[6,256,2,64]{1,3,2,0:T(8,128)(2,1)S(1)}, f32[6,2,256]{2,1,0:T(2,128)S(1)}, bf16[6,3328,2,64]{1,3,2,0:T(8,128)(2,1)}, bf16[6,256...) while((s32[]{:T(128)}, ...), condition=%wide.region_13.14_spmd.clone, body=%wide.region_10.13_spmd.clone.sunk | while | flops 451542528 | bytes 24085872 | solution.py:156
  800.8 11.1 fusion.133
  833.7 121.5 %while.58 = (s32[]{:T(128)}, f32[6,256,2,64]{1,3,2,0:T(8,128)}, f32[6,3328,2,64]{1,3,2,0:T(8,128)}, f32[6,3328,2,64]{1,3,2,0:T(8,128)}, bf16[6,3328,2,64]{1,3,2,...) while((s32[]{:T(128)}, f32[6,256,2,64]{1,3,2,0:T(8,128)}, ...), condition=%wide.region_20.21_spmd.clone, body=%wide.region_18.20_spmd.clone.sunk | while | flops 1107557888 | bytes 75987424 | solution.py:257
  955.2 10.0 fusion.91
  974.7 27.5 %collective-permute-start.39 = (bf16[256,1536]{0,1:T(8,128)(2,1)S(1)}, bf16[256,1536]{0,1:T(8,128)(2,1)S(1)}, u32[]{:S(2)}, u32[]{:S(2)}) collective-permute-start(bf16[256,1536]{0,1:T(8,128)(2,1)S(1)} %get-tuple-element.538), channel_id=1, source_target_pairs={{0,2},{1,3},{2,4},{3,5},{4,6},{5,7},{6,8},{7,9},{8,10},{9,11},{10,... | collective-permute-start | bytes 2359304 | tf_op jit(solution)/shard_map/ppermute | solution.py:16
  1003.5 12.2 collective-permute-start.41
  1017.0 66.7 %collective-permute-done.38 = bf16[256,1536]{0,1:T(8,128)(2,1)S(1)} collective-permute-done((bf16[256,1536]{0,1:T(8,128)(2,1)S(1)}, bf16[256,1536]{0,1:T(8,128)(2,1)S(1)}, u32[]{:S(2)}, u32[]{:S(2)}) %collective-permute-start.38) | collective-permute-done | bytes 786464 | tf_op jit(solution)/shard_map/ppermute | solution.py:16
  1100.7 48.4 %collective-permute-start.47 = (bf16[256,1536]{0,1:T(8,128)(2,1)S(1)}, bf16[256,1536]{0,1:T(8,128)(2,1)}, u32[]{:S(2)}, u32[]{:S(2)}) collective-permute-start(bf16[256,1536]{0,1:T(8,128)(2,1)S(1)} %get-tuple-element.530), channel_id=1, source_target_pairs={{0,6},{1,7},{2,8},{3,9},{4,10},{5,11},{6,12},{7,13},{8,14},{9,15},... | collective-permute-start | bytes 2359304 | tf_op jit(solution)/shard_map/ppermute | solution.py:16
  1152.7 35.9 %collective-permute-done.46 = bf16[256,1536]{0,1:T(8,128)(2,1)} collective-permute-done((bf16[256,1536]{0,1:T(8,128)(2,1)}, bf16[256,1536]{0,1:T(8,128)(2,1)}, u32[]{:S(2)}, u32[]{:S(2)}) %collective-permute-start.46) | collective-permute-done | bytes 786464 | tf_op jit(solution)/shard_map/ppermute | solution.py:16
  1219.3 126.5 %while.59 = (s32[]{:T(128)}, f32[6,256,2,64]{1,3,2,0:T(8,128)}, f32[6,3328,2,64]{1,3,2,0:T(8,128)}, f32[6,3328,2,64]{1,3,2,0:T(8,128)}, bf16[6,3328,2,64]{1,3,2,...) while((s32[]{:T(128)}, f32[6,256,2,64]{1,3,2,0:T(8,128)}, ...), condition=%wide.region_27.28_spmd.clone, body=%wide.region_25.27_spmd.clone.sunk | while | flops 1107557888 | bytes 75987424 | solution.py:257
  1350.3 16.8 fusion.90
  1372.8 8.7 collective-permute-start.49
  1382.8 23.1 collective-permute-start.51
  1407.3 12.2 collective-permute-start.53
  1420.8 66.4 %collective-permute-done.50 = bf16[256,1536]{0,1:T(8,128)(2,1)S(1)} collective-permute-done((bf16[256,1536]{0,1:T(8,128)(2,1)S(1)}, bf16[256,1536]{0,1:T(8,128)(2,1)S(1)}, u32[]{:S(2)}, u32[]{:S(2)}) %collective-permute-start.50) | collective-permute-done | bytes 786464 | tf_op jit(solution)/shard_map/ppermute | solution.py:16
  1495.6 15.5 collective-permute-start.57
  1512.4 49.2 %collective-permute-start.59 = (bf16[256,1536]{0,1:T(8,128)(2,1)S(1)}, bf16[256,1536]{0,1:T(8,128)(2,1)S(1)}, u32[]{:S(2)}, u32[]{:S(2)}) collective-permute-start(bf16[256,1536]{0,1:T(8,128)(2,1)S(1)} %get-tuple-element.518), channel_id=1, source_target_pairs={{0,6},{1,7},{2,8},{3,9},{4,10},{5,11},{6,12},{7,13},{8,14},{9,15},... | collective-permute-start | bytes 2359304 | tf_op jit(solution)/shard_map/ppermute | solution.py:16
  1563.0 20.7 collective-permute-done.58
  1630.0 85.8 %reduce-scatter.27.cloned.1.call-done = bf16[96,2304]{1,0:T(8,128)(2,1)} async-done(((bf16[768,2304]{1,0:T(8,128)(2,1)}), bf16[96,2304]{1,0:T(8,128)(2,1)}) %reduce-scatter.27.cloned.1.call-update) | async-done | bytes 442384 | tf_op jit(solution)/shard_map/reduce_scatter | solution.py:307
  1715.8 57.2 %reduce-scatter.37.cloned.1.call-done = bf16[96,3072]{1,0:T(8,128)(2,1)} async-done(((bf16[768,3072]{1,0:T(8,128)(2,1)}), bf16[96,3072]{1,0:T(8,128)(2,1)}) %reduce-scatter.37.cloned.1.call-update) | async-done | bytes 589840 | tf_op jit(solution)/shard_map/reduce_scatter | solution.py:316
  1773.0 57.1 %reduce-scatter.41.cloned.1.call-done = bf16[384,768]{1,0:T(8,128)(2,1)} async-done(((bf16[3072,768]{1,0:T(8,128)(2,1)}), bf16[384,768]{1,0:T(8,128)(2,1)}) %reduce-scatter.41.cloned.1.call-update) | async-done | bytes 589840 | tf_op jit(solution)/shard_map/reduce_scatter | solution.py:322
  1830.2 57.1 %reduce-scatter.39.cloned.1.call-done = bf16[384,768]{1,0:T(8,128)(2,1)} async-done(((bf16[3072,768]{1,0:T(8,128)(2,1)}), bf16[384,768]{1,0:T(8,128)(2,1)}) %reduce-scatter.39.cloned.1.call-update) | async-done | bytes 589840 | tf_op jit(solution)/shard_map/reduce_scatter | solution.py:322
  1887.3 57.1 %reduce-scatter.35.cloned.1.call-done = bf16[96,3072]{1,0:T(8,128)(2,1)} async-done(((bf16[768,3072]{1,0:T(8,128)(2,1)}), bf16[96,3072]{1,0:T(8,128)(2,1)}) %reduce-scatter.35.cloned.1.call-update) | async-done | bytes 589840 | tf_op jit(solution)/shard_map/reduce_scatter | solution.py:316
  1946.0 22.9 all-reduce.6
  1981.8 36.3 %reduce-scatter.49.cloned.1.call-done = bf16[96,2]{1,0:T(8,128)(2,1)} async-done(((bf16[768,2]{1,0:T(8,128)(2,1)}), bf16[96,2]{1,0:T(8,128)(2,1)}) %reduce-scatter.49.cloned.1.call-update) | async-done | bytes 400
  2018.9 36.5 %reduce-scatter.45.cloned.1.call-done = bf16[96,3]{1,0:T(8,128)(2,1)} async-done(((bf16[768,3]{1,0:T(8,128)(2,1)}), bf16[96,3]{1,0:T(8,128)(2,1)}) %reduce-scatter.45.cloned.1.call-update) | async-done | bytes 592
  2057.4 34.5 %reduce-scatter.51.cloned.1.call-done = bf16[96,2]{1,0:T(8,128)(2,1)} async-done(((bf16[768,2]{1,0:T(8,128)(2,1)}), bf16[96,2]{1,0:T(8,128)(2,1)}) %reduce-scatter.51.cloned.1.call-update) | async-done | bytes 400
  2092.7 35.9 %reduce-scatter.47.cloned.1.call-done = bf16[96,2]{1,0:T(8,128)(2,1)} async-done(((bf16[768,2]{1,0:T(8,128)(2,1)}), bf16[96,2]{1,0:T(8,128)(2,1)}) %reduce-scatter.47.cloned.1.call-update) | async-done | bytes 400
  2129.5 36.5 %reduce-scatter.43.cloned.1.call-done = bf16[96,3]{1,0:T(8,128)(2,1)} async-done(((bf16[768,3]{1,0:T(8,128)(2,1)}), bf16[96,3]{1,0:T(8,128)(2,1)}) %reduce-scatter.43.cloned.1.call-update) | async-done | bytes 592
  2166.8 11.9 all-reduce.7
  2181.6 121.3 %all-reduce.11.cloned.1.call-done = (bf16[1,96,2304]{2,1,0:T(8,128)(2,1)}, bf16[1,96,2304]{2,1,0:T(8,128)(2,1)}, bf16[1,96,768]{2,1,0:T(8,128)(2,1)}, bf16[1,96,...) async-done(((bf16[1,96,2304]{2,1,0:T(8,128)(2,1)}, ...) | async-done | bytes 3538960 | tf_op jit(solution)/shard_map/psum | solution.py:336
  (801 shorter events, 676.3 us)
Async XLA Ops:
  7.2 155.8 %all-gather.27.cloned.1.call-start = ((), (), s32[]{:S(2)}) async-start(), calls=%async_computation.22 | async-start | bytes 3981312 | tf_op jit(solution)/shard_map/all_gather | solution.py:100
  9.5 457.7 %all-gather.29.cloned.1.call-start = ((), (), s32[]{:S(2)}) async-start(), calls=%async_computation.23 | async-start | bytes 1327104 | tf_op jit(solution)/shard_map/all_gather | solution.py:102
  11.3 458.3 %all-gather.31.cloned.1.call-start = ((), (), s32[]{:S(2)}) async-start(), calls=%async_computation.24 | async-start | bytes 5308416 | tf_op jit(solution)/shard_map/all_gather | solution.py:103
  12.5 468.6 %all-gather.33.cloned.1.call-start = ((), (), s32[]{:S(2)}) async-start(), calls=%async_computation.25 | async-start | bytes 5308416 | tf_op jit(solution)/shard_map/all_gather | solution.py:105
  13.7 472.0 %all-gather.35.cloned.1.call-start = ((), (), s32[]{:S(2)}) async-start(), calls=%async_computation.26 | async-start | bytes 3981312 | tf_op jit(solution)/shard_map/all_gather | solution.py:100
  14.3 784.3 %all-gather.37.cloned.1.call-start = ((), (), s32[]{:S(2)}) async-start(), calls=%async_computation.27 | async-start | bytes 1327104 | tf_op jit(solution)/shard_map/all_gather | solution.py:102
  14.9 785.9 %all-gather.39.cloned.1.call-start = ((), (), s32[]{:S(2)}) async-start(), calls=%async_computation.28 | async-start | bytes 5308416 | tf_op jit(solution)/shard_map/all_gather | solution.py:103
  14.9 139.6 %collective-permute-start.12 = (s32[256]{0:T(256)S(1)}, s32[256]{0:T(256)S(1)}, u32[]{:S(2)}, u32[]{:S(2)}) collective-permute-start(s32[256]{0:T(256)S(1)} %broadcast_add_fusion), channel_id=1, source_target_pairs={{0,6},{1,7},{2,8},{3,9},{4,10},{5,11},{6,12},{7,13},{8,14},{9,15},... | collective-permute-start | bytes 3080 | tf_op jit(solution)/shard_map/ppermute | solution.py:16
  20.4 137.1 %collective-permute-start.13 = (s32[256]{0:T(256)S(1)}, s32[256]{0:T(256)S(1)}, u32[]{:S(2)}, u32[]{:S(2)}) collective-permute-start(s32[256]{0:T(256)S(1)} %broadcast_add_fusion), channel_id=1, source_target_pairs={{0,5},{1,6},{2,7},{3,8},{4,9},{5,10},{6,11},{7,12},{8,13},{9,14},{... | collective-permute-start | bytes 3080 | tf_op jit(solution)/shard_map/ppermute | solution.py:16
  25.0 133.7 %collective-permute-start.14 = (s32[256]{0:T(256)S(1)}, s32[256]{0:T(256)S(1)}, u32[]{:S(2)}, u32[]{:S(2)}) collective-permute-start(s32[256]{0:T(256)S(1)} %broadcast_add_fusion), channel_id=1, source_target_pairs={{0,4},{1,5},{2,6},{3,7},{4,8},{5,9},{6,10},{7,11},{8,12},{9,13},{1... | collective-permute-start | bytes 3080 | tf_op jit(solution)/shard_map/ppermute | solution.py:16
  26.8 133.3 %collective-permute-start.15 = (s32[256]{0:T(256)S(1)}, s32[256]{0:T(256)S(1)}, u32[]{:S(2)}, u32[]{:S(2)}) collective-permute-start(s32[256]{0:T(256)S(1)} %broadcast_add_fusion), channel_id=1, source_target_pairs={{0,3},{1,4},{2,5},{3,6},{4,7},{5,8},{6,9},{7,10},{8,11},{9,12},{10... | collective-permute-start | bytes 3080 | tf_op jit(solution)/shard_map/ppermute | solution.py:16
  32.2 129.3 %collective-permute-start.16 = (s32[256]{0:T(256)S(1)}, s32[256]{0:T(256)S(1)}, u32[]{:S(2)}, u32[]{:S(2)}) collective-permute-start(s32[256]{0:T(256)S(1)} %broadcast_add_fusion), channel_id=1, source_target_pairs={{0,2},{1,3},{2,4},{3,5},{4,6},{5,7},{6,8},{7,9},{8,10},{9,11},{10,... | collective-permute-start | bytes 3080 | tf_op jit(solution)/shard_map/ppermute | solution.py:16
  33.5 778.4 %all-gather.41.cloned.1.call-start = ((), (), s32[]{:S(2)}) async-start(), calls=%async_computation.29 | async-start | bytes 5308416 | tf_op jit(solution)/shard_map/all_gather | solution.py:105
  166.4 72.1 %collective-permute-start = (bf16[256,1536]{1,0:T(8,128)(2,1)S(1)}, bf16[256,1536]{1,0:T(8,128)(2,1)}, u32[]{:S(2)}, u32[]{:S(2)}) collective-permute-start(bf16[256,1536]{1,0:T(8,128)(2,1)S(1)} %pad_maximum_fusion.4), channel_id=1, source_target_pairs={{0,6},{1,7},{2,8},{3,9},{4,10},{5,11},{6,12},{7,13},{8,14},{9,15},... | collective-permute-start | bytes 2359304 | tf_op jit(solution)/shard_map/ppermute | solution.py:16
  178.3 95.1 %collective-permute-start.1 = (bf16[256,1536]{1,0:T(8,128)(2,1)S(1)}, bf16[256,1536]{1,0:T(8,128)(2,1)}, u32[]{:S(2)}, u32[]{:S(2)}) collective-permute-start(bf16[256,1536]{1,0:T(8,128)(2,1)S(1)} %pad_maximum_fusion.4), channel_id=1, source_target_pairs={{0,5},{1,6},{2,7},{3,8},{4,9},{5,10},{6,11},{7,12},{8,13},{9,14},{... | collective-permute-start | bytes 2359304 | tf_op jit(solution)/shard_map/ppermute | solution.py:16
  186.7 90.1 %collective-permute-start.2 = (bf16[256,1536]{1,0:T(8,128)(2,1)S(1)}, bf16[256,1536]{1,0:T(8,128)(2,1)}, u32[]{:S(2)}, u32[]{:S(2)}) collective-permute-start(bf16[256,1536]{1,0:T(8,128)(2,1)S(1)} %pad_maximum_fusion.4), channel_id=1, source_target_pairs={{0,4},{1,5},{2,6},{3,7},{4,8},{5,9},{6,10},{7,11},{8,12},{9,13},{1... | collective-permute-start | bytes 2359304 | tf_op jit(solution)/shard_map/ppermute | solution.py:16
  190.0 90.2 %collective-permute-start.3 = (bf16[256,1536]{1,0:T(8,128)(2,1)S(1)}, bf16[256,1536]{1,0:T(8,128)(2,1)}, u32[]{:S(2)}, u32[]{:S(2)}) collective-permute-start(bf16[256,1536]{1,0:T(8,128)(2,1)S(1)} %pad_maximum_fusion.4), channel_id=1, source_target_pairs={{0,3},{1,4},{2,5},{3,6},{4,7},{5,8},{6,9},{7,10},{8,11},{9,12},{10... | collective-permute-start | bytes 2359304 | tf_op jit(solution)/shard_map/ppermute | solution.py:16
  276.8 102.6 %collective-permute-start.7 = (bf16[256,1536]{1,0:T(8,128)(2,1)S(1)}, bf16[256,1536]{1,0:T(8,128)(2,1)S(1)}, u32[]{:S(2)}, u32[]{:S(2)}) collective-permute-start(bf16[256,1536]{1,0:T(8,128)(2,1)S(1)} %pad_maximum_fusion.4), channel_id=1, source_target_pairs={{2,0},{3,1},{4,2},{5,3},{6,4},{7,5},{8,6},{9,7},{10,8},{11,9},{12,... | collective-permute-start | bytes 2359304 | tf_op jit(solution)/shard_map/ppermute | solution.py:16
  280.2 100.2 %collective-permute-start.8 = (bf16[256,1536]{1,0:T(8,128)(2,1)S(1)}, bf16[256,1536]{1,0:T(8,128)(2,1)S(1)}, u32[]{:S(2)}, u32[]{:S(2)}) collective-permute-start(bf16[256,1536]{1,0:T(8,128)(2,1)S(1)} %pad_maximum_fusion.4), channel_id=1, source_target_pairs={{3,0},{4,1},{5,2},{6,3},{7,4},{8,5},{9,6},{10,7},{11,8},{12,9},{13... | collective-permute-start | bytes 2359304 | tf_op jit(solution)/shard_map/ppermute | solution.py:16
  283.6 97.8 %collective-permute-start.9 = (bf16[256,1536]{1,0:T(8,128)(2,1)S(1)}, bf16[256,1536]{1,0:T(8,128)(2,1)S(1)}, u32[]{:S(2)}, u32[]{:S(2)}) collective-permute-start(bf16[256,1536]{1,0:T(8,128)(2,1)S(1)} %pad_maximum_fusion.4), channel_id=1, source_target_pairs={{4,0},{5,1},{6,2},{7,3},{8,4},{9,5},{10,6},{11,7},{12,8},{13,9},{1... | collective-permute-start | bytes 2359304 | tf_op jit(solution)/shard_map/ppermute | solution.py:16
  289.2 93.1 %collective-permute-start.10 = (bf16[256,1536]{1,0:T(8,128)(2,1)S(1)}, bf16[256,1536]{1,0:T(8,128)(2,1)S(1)}, u32[]{:S(2)}, u32[]{:S(2)}) collective-permute-start(bf16[256,1536]{1,0:T(8,128)(2,1)S(1)} %pad_maximum_fusion.4), channel_id=1, source_target_pairs={{5,0},{6,1},{7,2},{8,3},{9,4},{10,5},{11,6},{12,7},{13,8},{14,9},{... | collective-permute-start | bytes 2359304 | tf_op jit(solution)/shard_map/ppermute | solution.py:16
  310.9 85.0 %collective-permute-start.11 = (bf16[256,1536]{1,0:T(8,128)(2,1)S(1)}, bf16[256,1536]{1,0:T(8,128)(2,1)S(1)}, u32[]{:S(2)}, u32[]{:S(2)}) collective-permute-start(bf16[256,1536]{1,0:T(8,128)(2,1)S(1)} %pad_maximum_fusion.4), channel_id=1, source_target_pairs={{6,0},{7,1},{8,2},{9,3},{10,4},{11,5},{12,6},{13,7},{14,8},{15,9},... | collective-permute-start | bytes 2359304 | tf_op jit(solution)/shard_map/ppermute | solution.py:16
  489.2 92.2 %collective-permute-start.24 = (bf16[256,1536]{1,0:T(8,128)(2,1)S(1)}, bf16[256,1536]{1,0:T(8,128)(2,1)}, u32[]{:S(2)}, u32[]{:S(2)}) collective-permute-start(bf16[256,1536]{1,0:T(8,128)(2,1)S(1)} %pad_maximum_fusion.5), channel_id=1, source_target_pairs={{0,6},{1,7},{2,8},{3,9},{4,10},{5,11},{6,12},{7,13},{8,14},{9,15},... | collective-permute-start | bytes 2359304 | tf_op jit(solution)/shard_map/ppermute | solution.py:16
  506.7 78.1 %collective-permute-start.25 = (bf16[256,1536]{1,0:T(8,128)(2,1)S(1)}, bf16[256,1536]{1,0:T(8,128)(2,1)}, u32[]{:S(2)}, u32[]{:S(2)}) collective-permute-start(bf16[256,1536]{1,0:T(8,128)(2,1)S(1)} %pad_maximum_fusion.5), channel_id=1, source_target_pairs={{0,5},{1,6},{2,7},{3,8},{4,9},{5,10},{6,11},{7,12},{8,13},{9,14},{... | collective-permute-start | bytes 2359304 | tf_op jit(solution)/shard_map/ppermute | solution.py:16
  521.2 67.0 %collective-permute-start.26 = (bf16[256,1536]{1,0:T(8,128)(2,1)S(1)}, bf16[256,1536]{1,0:T(8,128)(2,1)}, u32[]{:S(2)}, u32[]{:S(2)}) collective-permute-start(bf16[256,1536]{1,0:T(8,128)(2,1)S(1)} %pad_maximum_fusion.5), channel_id=1, source_target_pairs={{0,4},{1,5},{2,6},{3,7},{4,8},{5,9},{6,10},{7,11},{8,12},{9,13},{1... | collective-permute-start | bytes 2359304 | tf_op jit(solution)/shard_map/ppermute | solution.py:16
  523.4 68.3 %collective-permute-start.27 = (bf16[256,1536]{1,0:T(8,128)(2,1)S(1)}, bf16[256,1536]{1,0:T(8,128)(2,1)}, u32[]{:S(2)}, u32[]{:S(2)}) collective-permute-start(bf16[256,1536]{1,0:T(8,128)(2,1)S(1)} %pad_maximum_fusion.5), channel_id=1, source_target_pairs={{0,3},{1,4},{2,5},{3,6},{4,7},{5,8},{6,9},{7,10},{8,11},{9,12},{10... | collective-permute-start | bytes 2359304 | tf_op jit(solution)/shard_map/ppermute | solution.py:16
  529.0 1101.0 %reduce-scatter.33.cloned.1.call-start = ((), (), s32[]{:S(2)}) async-start(), calls=%async_computation.17 | async-start | bytes 1327104 | tf_op jit(solution)/shard_map/reduce_scatter | solution.py:313
  588.2 125.5 %collective-permute-start.31 = (bf16[256,1536]{1,0:T(8,128)(2,1)S(1)}, bf16[256,1536]{1,0:T(8,128)(2,1)S(1)}, u32[]{:S(2)}, u32[]{:S(2)}) collective-permute-start(bf16[256,1536]{1,0:T(8,128)(2,1)S(1)} %pad_maximum_fusion.5), channel_id=1, source_target_pairs={{2,0},{3,1},{4,2},{5,3},{6,4},{7,5},{8,6},{9,7},{10,8},{11,9},{12,... | collective-permute-start | bytes 2359304 | tf_op jit(solution)/shard_map/ppermute | solution.py:16
  591.6 123.0 %collective-permute-start.32 = (bf16[256,1536]{1,0:T(8,128)(2,1)S(1)}, bf16[256,1536]{1,0:T(8,128)(2,1)S(1)}, u32[]{:S(2)}, u32[]{:S(2)}) collective-permute-start(bf16[256,1536]{1,0:T(8,128)(2,1)S(1)} %pad_maximum_fusion.5), channel_id=1, source_target_pairs={{3,0},{4,1},{5,2},{6,3},{7,4},{8,5},{9,6},{10,7},{11,8},{12,9},{13... | collective-permute-start | bytes 2359304 | tf_op jit(solution)/shard_map/ppermute | solution.py:16
  598.2 117.4 %collective-permute-start.33 = (bf16[256,1536]{1,0:T(8,128)(2,1)S(1)}, bf16[256,1536]{1,0:T(8,128)(2,1)S(1)}, u32[]{:S(2)}, u32[]{:S(2)}) collective-permute-start(bf16[256,1536]{1,0:T(8,128)(2,1)S(1)} %pad_maximum_fusion.5), channel_id=1, source_target_pairs={{4,0},{5,1},{6,2},{7,3},{8,4},{9,5},{10,6},{11,7},{12,8},{13,9},{1... | collective-permute-start | bytes 2359304 | tf_op jit(solution)/shard_map/ppermute | solution.py:16
  615.0 101.5 %collective-permute-start.34 = (bf16[256,1536]{1,0:T(8,128)(2,1)S(1)}, bf16[256,1536]{1,0:T(8,128)(2,1)S(1)}, u32[]{:S(2)}, u32[]{:S(2)}) collective-permute-start(bf16[256,1536]{1,0:T(8,128)(2,1)S(1)} %pad_maximum_fusion.5), channel_id=1, source_target_pairs={{5,0},{6,1},{7,2},{8,3},{9,4},{10,5},{11,6},{12,7},{13,8},{14,9},{... | collective-permute-start | bytes 2359304 | tf_op jit(solution)/shard_map/ppermute | solution.py:16
  626.6 100.9 %collective-permute-start.35 = (bf16[256,1536]{1,0:T(8,128)(2,1)S(1)}, bf16[256,1536]{1,0:T(8,128)(2,1)S(1)}, u32[]{:S(2)}, u32[]{:S(2)}) collective-permute-start(bf16[256,1536]{1,0:T(8,128)(2,1)S(1)} %pad_maximum_fusion.5), channel_id=1, source_target_pairs={{6,0},{7,1},{8,2},{9,3},{10,4},{11,5},{12,6},{13,7},{14,8},{15,9},... | collective-permute-start | bytes 2359304 | tf_op jit(solution)/shard_map/ppermute | solution.py:16
  973.4 110.3 %collective-permute-start.38 = (bf16[256,1536]{0,1:T(8,128)(2,1)S(1)}, bf16[256,1536]{0,1:T(8,128)(2,1)S(1)}, u32[]{:S(2)}, u32[]{:S(2)}) collective-permute-start(bf16[256,1536]{0,1:T(8,128)(2,1)S(1)} %get-tuple-element.539), channel_id=1, source_target_pairs={{2,0},{3,1},{4,2},{5,3},{6,4},{7,5},{8,6},{9,7},{10,8},{11,9},{12,... | collective-permute-start | bytes 2359304 | tf_op jit(solution)/shard_map/ppermute | solution.py:16
  974.7 116.4 %collective-permute-start.39 = (bf16[256,1536]{0,1:T(8,128)(2,1)S(1)}, bf16[256,1536]{0,1:T(8,128)(2,1)S(1)}, u32[]{:S(2)}, u32[]{:S(2)}) collective-permute-start(bf16[256,1536]{0,1:T(8,128)(2,1)S(1)} %get-tuple-element.538), channel_id=1, source_target_pairs={{0,2},{1,3},{2,4},{3,5},{4,6},{5,7},{6,8},{7,9},{8,10},{9,11},{10,... | collective-permute-start | bytes 2359304 | tf_op jit(solution)/shard_map/ppermute | solution.py:16
  1002.2 90.2 %collective-permute-start.40 = (bf16[256,1536]{0,1:T(8,128)(2,1)S(1)}, bf16[256,1536]{0,1:T(8,128)(2,1)S(1)}, u32[]{:S(2)}, u32[]{:S(2)}) collective-permute-start(bf16[256,1536]{0,1:T(8,128)(2,1)S(1)} %get-tuple-element.537), channel_id=1, source_target_pairs={{3,0},{4,1},{5,2},{6,3},{7,4},{8,5},{9,6},{10,7},{11,8},{12,9},{13... | collective-permute-start | bytes 2359304 | tf_op jit(solution)/shard_map/ppermute | solution.py:16
  1003.5 95.8 %collective-permute-start.41 = (bf16[256,1536]{0,1:T(8,128)(2,1)S(1)}, bf16[256,1536]{0,1:T(8,128)(2,1)S(1)}, u32[]{:S(2)}, u32[]{:S(2)}) collective-permute-start(bf16[256,1536]{0,1:T(8,128)(2,1)S(1)} %get-tuple-element.536), channel_id=1, source_target_pairs={{0,3},{1,4},{2,5},{3,6},{4,7},{5,8},{6,9},{7,10},{8,11},{9,12},{10... | collective-permute-start | bytes 2359304 | tf_op jit(solution)/shard_map/ppermute | solution.py:16
  1015.7 84.9 %collective-permute-start.42 = (bf16[256,1536]{0,1:T(8,128)(2,1)S(1)}, bf16[256,1536]{0,1:T(8,128)(2,1)S(1)}, u32[]{:S(2)}, u32[]{:S(2)}) collective-permute-start(bf16[256,1536]{0,1:T(8,128)(2,1)S(1)} %get-tuple-element.535), channel_id=1, source_target_pairs={{4,0},{5,1},{6,2},{7,3},{8,4},{9,5},{10,6},{11,7},{12,8},{13,9},{1... | collective-permute-start | bytes 2359304 | tf_op jit(solution)/shard_map/ppermute | solution.py:16
  1083.7 69.0 %collective-permute-start.43 = (bf16[256,1536]{0,1:T(8,128)(2,1)}, bf16[256,1536]{0,1:T(8,128)(2,1)}, u32[]{:S(2)}, u32[]{:S(2)}) collective-permute-start(bf16[256,1536]{0,1:T(8,128)(2,1)} %get-tuple-element.534), channel_id=1, source_target_pairs={{0,4},{1,5},{2,6},{3,7},{4,8},{5,9},{6,10},{7,11},{8,12},{9,13},{1... | collective-permute-start | bytes 2359304 | tf_op jit(solution)/shard_map/ppermute | solution.py:16
  1099.4 89.2 %collective-permute-start.46 = (bf16[256,1536]{0,1:T(8,128)(2,1)}, bf16[256,1536]{0,1:T(8,128)(2,1)}, u32[]{:S(2)}, u32[]{:S(2)}) collective-permute-start(bf16[256,1536]{0,1:T(8,128)(2,1)} %get-tuple-element.531), channel_id=1, source_target_pairs={{6,0},{7,1},{8,2},{9,3},{10,4},{11,5},{12,6},{13,7},{14,8},{15,9},... | collective-permute-start | bytes 2359304 | tf_op jit(solution)/shard_map/ppermute | solution.py:16
  1100.7 87.9 %collective-permute-start.47 = (bf16[256,1536]{0,1:T(8,128)(2,1)S(1)}, bf16[256,1536]{0,1:T(8,128)(2,1)}, u32[]{:S(2)}, u32[]{:S(2)}) collective-permute-start(bf16[256,1536]{0,1:T(8,128)(2,1)S(1)} %get-tuple-element.530), channel_id=1, source_target_pairs={{0,6},{1,7},{2,8},{3,9},{4,10},{5,11},{6,12},{7,13},{8,14},{9,15},... | collective-permute-start | bytes 2359304 | tf_op jit(solution)/shard_map/ppermute | solution.py:16
  1150.7 479.3 %reduce-scatter.31.cloned.1.call-start = ((), (), s32[]{:S(2)}) async-start(), calls=%async_computation.16 | async-start | bytes 1327104 | tf_op jit(solution)/shard_map/reduce_scatter | solution.py:313
  1208.7 421.3 %reduce-scatter.29.cloned.1.call-start = ((), (), s32[]{:S(2)}) async-start(), calls=%async_computation.15 | async-start | bytes 3981312 | tf_op jit(solution)/shard_map/reduce_scatter | solution.py:307
  1350.2 365.6 %reduce-scatter.27.cloned.1.call-start = ((), (), s32[]{:S(2)}) async-start(), calls=%async_computation.14 | async-start | bytes 3981312 | tf_op jit(solution)/shard_map/reduce_scatter | solution.py:307
  1381.5 105.7 %collective-permute-start.50 = (bf16[256,1536]{0,1:T(8,128)(2,1)S(1)}, bf16[256,1536]{0,1:T(8,128)(2,1)S(1)}, u32[]{:S(2)}, u32[]{:S(2)}) collective-permute-start(bf16[256,1536]{0,1:T(8,128)(2,1)S(1)} %get-tuple-element.527), channel_id=1, source_target_pairs={{2,0},{3,1},{4,2},{5,3},{6,4},{7,5},{8,6},{9,7},{10,8},{11,9},{12,... | collective-permute-start | bytes 2359304 | tf_op jit(solution)/shard_map/ppermute | solution.py:16
  1382.8 111.4 %collective-permute-start.51 = (bf16[256,1536]{0,1:T(8,128)(2,1)S(1)}, bf16[256,1536]{0,1:T(8,128)(2,1)S(1)}, u32[]{:S(2)}, u32[]{:S(2)}) collective-permute-start(bf16[256,1536]{0,1:T(8,128)(2,1)S(1)} %get-tuple-element.526), channel_id=1, source_target_pairs={{0,2},{1,3},{2,4},{3,5},{4,6},{5,7},{6,8},{7,9},{8,10},{9,11},{10,... | collective-permute-start | bytes 2359304 | tf_op jit(solution)/shard_map/ppermute | solution.py:16
  1406.0 89.6 %collective-permute-start.52 = (bf16[256,1536]{0,1:T(8,128)(2,1)S(1)}, bf16[256,1536]{0,1:T(8,128)(2,1)S(1)}, u32[]{:S(2)}, u32[]{:S(2)}) collective-permute-start(bf16[256,1536]{0,1:T(8,128)(2,1)S(1)} %get-tuple-element.525), channel_id=1, source_target_pairs={{3,0},{4,1},{5,2},{6,3},{7,4},{8,5},{9,6},{10,7},{11,8},{12,9},{13... | collective-permute-start | bytes 2359304 | tf_op jit(solution)/shard_map/ppermute | solution.py:16
  1407.3 103.8 %collective-permute-start.53 = (bf16[256,1536]{0,1:T(8,128)(2,1)S(1)}, bf16[256,1536]{0,1:T(8,128)(2,1)S(1)}, u32[]{:S(2)}, u32[]{:S(2)}) collective-permute-start(bf16[256,1536]{0,1:T(8,128)(2,1)S(1)} %get-tuple-element.524), channel_id=1, source_target_pairs={{0,3},{1,4},{2,5},{3,6},{4,7},{5,8},{6,9},{7,10},{8,11},{9,12},{10... | collective-permute-start | bytes 2359304 | tf_op jit(solution)/shard_map/ppermute | solution.py:16
  1419.5 92.9 %collective-permute-start.54 = (bf16[256,1536]{0,1:T(8,128)(2,1)S(1)}, bf16[256,1536]{0,1:T(8,128)(2,1)S(1)}, u32[]{:S(2)}, u32[]{:S(2)}) collective-permute-start(bf16[256,1536]{0,1:T(8,128)(2,1)S(1)} %get-tuple-element.523), channel_id=1, source_target_pairs={{4,0},{5,1},{6,2},{7,3},{8,4},{9,5},{10,6},{11,7},{12,8},{13,9},{1... | collective-permute-start | bytes 2359304 | tf_op jit(solution)/shard_map/ppermute | solution.py:16
  1487.2 75.8 %collective-permute-start.55 = (bf16[256,1536]{0,1:T(8,128)(2,1)S(1)}, bf16[256,1536]{0,1:T(8,128)(2,1)S(1)}, u32[]{:S(2)}, u32[]{:S(2)}) collective-permute-start(bf16[256,1536]{0,1:T(8,128)(2,1)S(1)} %get-tuple-element.522), channel_id=1, source_target_pairs={{0,4},{1,5},{2,6},{3,7},{4,8},{5,9},{6,10},{7,11},{8,12},{9,13},{1... | collective-permute-start | bytes 2359304 | tf_op jit(solution)/shard_map/ppermute | solution.py:16
  1494.3 68.7 %collective-permute-start.56 = (bf16[256,1536]{0,1:T(8,128)(2,1)S(1)}, bf16[256,1536]{0,1:T(8,128)(2,1)S(1)}, u32[]{:S(2)}, u32[]{:S(2)}) collective-permute-start(bf16[256,1536]{0,1:T(8,128)(2,1)S(1)} %get-tuple-element.521), channel_id=1, source_target_pairs={{5,0},{6,1},{7,2},{8,3},{9,4},{10,5},{11,6},{12,7},{13,8},{14,9},{... | collective-permute-start | bytes 2359304 | tf_op jit(solution)/shard_map/ppermute | solution.py:16
  1495.6 67.4 %collective-permute-start.57 = (bf16[256,1536]{0,1:T(8,128)(2,1)S(1)}, bf16[256,1536]{0,1:T(8,128)(2,1)S(1)}, u32[]{:S(2)}, u32[]{:S(2)}) collective-permute-start(bf16[256,1536]{0,1:T(8,128)(2,1)S(1)} %get-tuple-element.520), channel_id=1, source_target_pairs={{0,5},{1,6},{2,7},{3,8},{4,9},{5,10},{6,11},{7,12},{8,13},{9,14},{... | collective-permute-start | bytes 2359304 | tf_op jit(solution)/shard_map/ppermute | solution.py:16
  1511.1 72.6 %collective-permute-start.58 = (bf16[256,1536]{0,1:T(8,128)(2,1)S(1)}, bf16[256,1536]{0,1:T(8,128)(2,1)S(1)}, u32[]{:S(2)}, u32[]{:S(2)}) collective-permute-start(bf16[256,1536]{0,1:T(8,128)(2,1)S(1)} %get-tuple-element.519), channel_id=1, source_target_pairs={{6,0},{7,1},{8,2},{9,3},{10,4},{11,5},{12,6},{13,7},{14,8},{15,9},... | collective-permute-start | bytes 2359304 | tf_op jit(solution)/shard_map/ppermute | solution.py:16
  1512.4 71.4 %collective-permute-start.59 = (bf16[256,1536]{0,1:T(8,128)(2,1)S(1)}, bf16[256,1536]{0,1:T(8,128)(2,1)S(1)}, u32[]{:S(2)}, u32[]{:S(2)}) collective-permute-start(bf16[256,1536]{0,1:T(8,128)(2,1)S(1)} %get-tuple-element.518), channel_id=1, source_target_pairs={{0,6},{1,7},{2,8},{3,9},{4,10},{5,11},{6,12},{7,13},{8,14},{9,15},... | collective-permute-start | bytes 2359304 | tf_op jit(solution)/shard_map/ppermute | solution.py:16
  1593.7 179.3 %reduce-scatter.37.cloned.1.call-start = ((), (), s32[]{:S(2)}) async-start(), calls=%async_computation.19 | async-start | bytes 5308416 | tf_op jit(solution)/shard_map/reduce_scatter | solution.py:316
  1600.1 230.1 %reduce-scatter.41.cloned.1.call-start = ((), (), s32[]{:S(2)}) async-start(), calls=%async_computation.21 | async-start | bytes 5308416 | tf_op jit(solution)/shard_map/reduce_scatter | solution.py:322
  1606.1 281.2 %reduce-scatter.39.cloned.1.call-start = ((), (), s32[]{:S(2)}) async-start(), calls=%async_computation.20 | async-start | bytes 5308416 | tf_op jit(solution)/shard_map/reduce_scatter | solution.py:322
  1611.5 332.9 %reduce-scatter.35.cloned.1.call-start = ((), (), s32[]{:S(2)}) async-start(), calls=%async_computation.18 | async-start | bytes 5308416 | tf_op jit(solution)/shard_map/reduce_scatter | solution.py:316
  1617.3 363.7 %reduce-scatter.53.cloned.1.call-start = ((), (), s32[]{:S(2)}) async-start(), calls=%async_computation.35 | async-start | bytes 221184
  1620.3 397.8 %reduce-scatter.49.cloned.1.call-start = ((), (), s32[]{:S(2)}) async-start(), calls=%async_computation.33 | async-start | bytes 221184
  1621.2 434.2 %reduce-scatter.45.cloned.1.call-start = ((), (), s32[]{:S(2)}) async-start(), calls=%async_computation.31 | async-start | bytes 221184
  1622.3 469.7 %reduce-scatter.51.cloned.1.call-start = ((), (), s32[]{:S(2)}) async-start(), calls=%async_computation.34 | async-start | bytes 221184
  1627.8 500.9 %reduce-scatter.47.cloned.1.call-start = ((), (), s32[]{:S(2)}) async-start(), calls=%async_computation.32 | async-start | bytes 221184
  1628.7 537.2 %reduce-scatter.43.cloned.1.call-start = ((), (), s32[]{:S(2)}) async-start(), calls=%async_computation.30 | async-start | bytes 221184
  1629.7 673.2 %all-reduce.11.cloned.1.call-start = ((), (), s32[]{:S(2)}) async-start(), calls=%async_computation.36 | async-start | bytes 7077888 | tf_op jit(solution)/shard_map/psum | solution.py:336
  (167 other events, 7498.1 us)
Sparse Core Ops, SparseCore 0:
  10.5 38.1 all-gather.26
  50.5 24.4 all-gather.28
  77.5 40.9 all-gather.30
  120.8 38.9 all-gather.32
  162.1 33.7 all-gather.34
  197.6 56.4 all-gather.36
  256.6 47.6 all-gather.38
  529.1 74.4 all-gather.40
  1150.8 48.1 reduce-scatter.32
  1208.8 77.4 reduce-scatter.30
  1350.3 98.4 reduce-scatter.28
  1593.9 121.8 reduce-scatter.26
  1719.2 53.7 reduce-scatter.36
  1776.3 53.7 reduce-scatter.40
  1833.5 53.7 reduce-scatter.38
  1890.6 53.7 reduce-scatter.34
  1947.2 33.6 reduce-scatter.52
  1984.4 33.6 reduce-scatter.48
  2021.7 33.6 reduce-scatter.44
  2058.2 33.6 reduce-scatter.50
  2095.0 33.6 reduce-scatter.46
  2132.2 33.6 reduce-scatter.42
  2168.9 133.9 all-reduce.10
where the time goes:
time: 2330 us; the launch traced here: 2320 us
  waiting for transfers between devices  1060 us (45%)
  starting transfers between devices  398 us (17%)
  matrix products  349 us (15%)
  other arithmetic  174 us (7%)
  blocking collectives  168 us (7%)
  local copies, waits for them, and re-layouts  143 us (6%)
    ppermute x60, waiting for transfers between devices, passed_along(): lax.ppermute(value, axis, [(source, source + steps) for source in range(l...  440 us
    ppermute x60, starting transfers between devices, passed_along(): lax.ppermute(value, axis, [(source, source + steps) for source in range(l...  397 us
    unnamed x29, waiting for transfers between devices  188 us
    psum x1, waiting for transfers between devices, local(): lax.psum(summed[0].astype(jnp.bfloat16), 'rep').astype(jnp.float32)  121 us
    reduce_scatter x2, waiting for transfers between devices, local(): lax.psum_scatter(grads[3].astype(jnp.bfloat16), 'group', scatter_dimensio...  114 us
    reduce_scatter x2, waiting for transfers between devices, local(): lax.psum_scatter(grads[5].astype(jnp.bfloat16), 'group', scatter_dimensio...  114 us
    reduce_scatter x2, waiting for transfers between devices, local(): lax.psum_scatter(grads[0].astype(jnp.bfloat16), 'group', scatter_dimensio...  85.8 us
    all_gather x2, blocking collectives, local(): lax.all_gather(fc1_bias[layer_at], 'group', axis=0, tiled=True)  58.5 us
  transfers between devices with their start and end apart: 83, of which 26 were waited for; matrix products, arithmetic and copies ran while one was open for 21% of the time, Pallas kernels for 0%

commit v1 on v0

--- a/solution.py
+++ b/solution.py
@@ -333,7 +333,7 @@
             ).astype(jnp.float32),
         )
         summed = (
-            lax.psum(summed[0].astype(jnp.bfloat16), "rep").astype(jnp.float32),
+            lax.all_gather(summed[0].astype(jnp.bfloat16), "rep").sum(axis=0).astype(jnp.float32),
             lax.psum(summed[1].astype(jnp.bfloat16), "rep").astype(jnp.float32),
             lax.psum(summed[2].astype(jnp.bfloat16), "rep").astype(jnp.float32),
             lax.psum(summed[3].astype(jnp.bfloat16), "rep").astype(jnp.float32),

time: 2330 us -> 2470 us (1.060)
  waiting for transfers between devices: 1060 us -> 1190 us
    reduce_scatter x2, waiting for transfers between devices: 0.04 us -> 79.7 us  [local(): lax.psum_scatter(grads[2].astype(jnp.bfloat16), 'group', scatter_dimensio...]
    all_gather x0 -> x2, waiting for transfers between devices: none -> 65 us  [local(): lax.all_gather(summed[0].astype(jnp.bfloat16), 'rep').sum(axis=0)]
    unnamed x284 -> x298, local copies, waits for them, and re-layouts: 53.4 us -> 54.4 us
    unnamed x29 -> x31, waiting for transfers between devices: 188 us -> 188 us
  transfers between devices with their start and end apart: 83 -> 85, of which waited for: 26 -> 30; matrix products, arithmetic and copies ran while one was open for 21% -> 14% of each run, Pallas kernels for 0% -> 0%
where the time goes in v1:
time: 2470 us; the launch traced here: 2450 us
  waiting for transfers between devices  1190 us (48%)
  starting transfers between devices  399 us (16%)
  matrix products  346 us (14%)
  other arithmetic  182 us (7%)
  blocking collectives  168 us (7%)
  local copies, waits for them, and re-layouts  150 us (6%)
    ppermute x60, waiting for transfers between devices, passed_along(): lax.ppermute(value, axis, [(source, source + steps) for source in range(l...  441 us
    ppermute x60, starting transfers between devices, passed_along(): lax.ppermute(value, axis, [(source, source + steps) for source in range(l...  398 us
    unnamed x31, waiting for transfers between devices  188 us
    reduce_scatter x2, waiting for transfers between devices, local(): lax.psum_scatter(grads[3].astype(jnp.bfloat16), 'group', scatter_dimensio...  114 us
    reduce_scatter x2, waiting for transfers between devices, local(): lax.psum_scatter(grads[5].astype(jnp.bfloat16), 'group', scatter_dimensio...  114 us
    psum x1, waiting for transfers between devices, local(): lax.psum(summed[2].astype(jnp.bfloat16), 'rep').astype(jnp.float32)  104 us
    reduce_scatter x2, waiting for transfers between devices, local(): lax.psum_scatter(grads[2].astype(jnp.bfloat16), 'group', scatter_dimensio...  79.7 us
    reduce_scatter x2, waiting for transfers between devices, local(): lax.psum_scatter(grads[0].astype(jnp.bfloat16), 'group', scatter_dimensio...  79 us
  transfers between devices with their start and end apart: 85, of which 30 were waited for; matrix products, arithmetic and copies ran while one was open for 14% of the time, Pallas kernels for 0%

profile of v1, /device:TPU:0, one launch (start us, length us, event | category | flops | bytes accessed | tf_op | source)
XLA Modules:
  0.0 2451.6 jit_solution(17659904451931129895)
XLA Ops:
  34.2 12.0 all-gather
  51.0 8.5 all-gather.1
  64.3 10.5 all-gather.3
  74.9 7.8 fusion.231
  82.7 8.5 all-gather.6
  91.9 9.2 all-gather.9
  105.9 11.3 all-gather.10
  121.9 9.2 all-gather.12
  131.1 7.8 fusion.224
  140.5 14.0 all-reduce
  166.4 10.5 collective-permute-start
  190.0 8.9 collective-permute-start.3
  198.9 30.8 %collective-permute-done.23 = s32[256]{0:T(256)S(1)} collective-permute-done((s32[256]{0:T(256)S(1)}, s32[256]{0:T(256)S(1)}, u32[]{:S(2)}, u32[]{:S(2)}) %collective-permute-start.23) | collective-permute-done | bytes 1056 | tf_op jit(solution)/shard_map/ppermute | solution.py:16
  229.7 8.7 collective-permute-start.4
  238.5 32.8 %collective-permute-start.5 = (bf16[256,1536]{1,0:T(8,128)(2,1)S(1)}, bf16[256,1536]{1,0:T(8,128)(2,1)S(1)}, u32[]{:S(2)}, u32[]{:S(2)}) collective-permute-start(bf16[256,1536]{1,0:T(8,128)(2,1)S(1)} %pad_maximum_fusion.4), channel_id=1, source_target_pairs={{0,1},{1,2},{2,3},{3,4},{4,5},{5,6},{6,7},{7,8},{8,9},{9,10},{10,1... | collective-permute-start | bytes 2359304 | tf_op jit(solution)/shard_map/ppermute | solution.py:16
  292.4 18.5 collective-permute-done.6
  313.1 66.3 %collective-permute-done.7 = bf16[256,1536]{1,0:T(8,128)(2,1)S(1)} collective-permute-done((bf16[256,1536]{1,0:T(8,128)(2,1)S(1)}, bf16[256,1536]{1,0:T(8,128)(2,1)S(1)}, u32[]{:S(2)}, u32[]{:S(2)}) %collective-permute-start.7) | collective-permute-done | bytes 786464 | tf_op jit(solution)/shard_map/ppermute | solution.py:16
  383.4 12.5 collective-permute-done.11
  396.9 8.4 fusion.258
  420.9 46.2 %while.56 = (s32[]{:T(128)}, bf16[6,256,2,64]{1,3,2,0:T(8,128)(2,1)S(1)}, f32[6,2,256]{2,1,0:T(2,128)S(1)}, bf16[6,3328,2,64]{1,3,2,0:T(8,128)(2,1)}, bf16[6,256...) while((s32[]{:T(128)}, ...), condition=%wide.region_5.6_spmd.clone, body=%wide.region_2.5_spmd.clone.sunk | while | flops 451542528 | bytes 24085872 | solution.py:156
  469.6 11.4 fusion.130
  489.6 17.4 collective-permute-start.24
  507.0 14.6 collective-permute-start.25
  529.5 50.1 %all-gather.15 = bf16[1,3072]{1,0:T(2,128)(2,1)S(1)} all-gather(bf16[1,384]{1,0:T(2,128)(2,1)S(1)} %get-tuple-element.561), channel_id=17, replica_groups=mesh['group'=8,'rep'=4] {'group'}, dimensions={1}, use_global_device_ids=true | all-gather | bytes 6912 | tf_op jit(solution)/shard_map/all_gather | solution.py:104
  602.1 13.5 collective-permute-done.29
  618.7 8.9 collective-permute-done.30
  629.8 84.4 %collective-permute-done.31 = bf16[256,1536]{1,0:T(8,128)(2,1)S(1)} collective-permute-done((bf16[256,1536]{1,0:T(8,128)(2,1)S(1)}, bf16[256,1536]{1,0:T(8,128)(2,1)S(1)}, u32[]{:S(2)}, u32[]{:S(2)}) %collective-permute-start.31) | collective-permute-done | bytes 786464 | tf_op jit(solution)/shard_map/ppermute | solution.py:16
  718.1 9.7 collective-permute-done.35
  728.8 8.4 fusion.257
  752.9 46.2 %while.57 = (s32[]{:T(128)}, bf16[6,256,2,64]{1,3,2,0:T(8,128)(2,1)S(1)}, f32[6,2,256]{2,1,0:T(2,128)S(1)}, bf16[6,3328,2,64]{1,3,2,0:T(8,128)(2,1)}, bf16[6,256...) while((s32[]{:T(128)}, ...), condition=%wide.region_13.14_spmd.clone, body=%wide.region_10.13_spmd.clone.sunk | while | flops 451542528 | bytes 24085872 | solution.py:156
  801.4 11.1 fusion.133
  834.6 118.1 %while.58 = (s32[]{:T(128)}, f32[6,256,2,64]{1,3,2,0:T(8,128)}, f32[6,3328,2,64]{1,3,2,0:T(8,128)}, f32[6,3328,2,64]{1,3,2,0:T(8,128)}, bf16[6,3328,2,64]{1,3,2,...) while((s32[]{:T(128)}, f32[6,256,2,64]{1,3,2,0:T(8,128)}, ...), condition=%wide.region_20.21_spmd.clone, body=%wide.region_18.20_spmd.clone.sunk | while | flops 1107557888 | bytes 72841640 | solution.py:257
  952.7 16.8 fusion.91
  981.3 27.5 %collective-permute-start.39 = (bf16[256,1536]{0,1:T(8,128)(2,1)S(1)}, bf16[256,1536]{0,1:T(8,128)(2,1)S(1)}, u32[]{:S(2)}, u32[]{:S(2)}) collective-permute-start(bf16[256,1536]{0,1:T(8,128)(2,1)S(1)} %get-tuple-element.536), channel_id=1, source_target_pairs={{0,2},{1,3},{2,4},{3,5},{4,6},{5,7},{6,8},{7,9},{8,10},{9,11},{10,... | collective-permute-start | bytes 2359304 | tf_op jit(solution)/shard_map/ppermute | solution.py:16
  1010.1 12.2 collective-permute-start.41
  1023.6 66.7 %collective-permute-done.38 = bf16[256,1536]{0,1:T(8,128)(2,1)S(1)} collective-permute-done((bf16[256,1536]{0,1:T(8,128)(2,1)S(1)}, bf16[256,1536]{0,1:T(8,128)(2,1)S(1)}, u32[]{:S(2)}, u32[]{:S(2)}) %collective-permute-start.38) | collective-permute-done | bytes 786464 | tf_op jit(solution)/shard_map/ppermute | solution.py:16
  1106.4 48.3 %collective-permute-start.47 = (bf16[256,1536]{0,1:T(8,128)(2,1)S(1)}, bf16[256,1536]{0,1:T(8,128)(2,1)S(1)}, u32[]{:S(2)}, u32[]{:S(2)}) collective-permute-start(bf16[256,1536]{0,1:T(8,128)(2,1)S(1)} %get-tuple-element.528), channel_id=1, source_target_pairs={{0,6},{1,7},{2,8},{3,9},{4,10},{5,11},{6,12},{7,13},{8,14},{9,15},... | collective-permute-start | bytes 2359304 | tf_op jit(solution)/shard_map/ppermute | solution.py:16
  1156.7 37.8 %collective-permute-done.46 = bf16[256,1536]{0,1:T(8,128)(2,1)S(1)} collective-permute-done((bf16[256,1536]{0,1:T(8,128)(2,1)S(1)}, bf16[256,1536]{0,1:T(8,128)(2,1)S(1)}, u32[]{:S(2)}, u32[]{:S(2)}) %collective-permute-start.46) | collective-permute-done | bytes 786464 | tf_op jit(solution)/shard_map/ppermute | solution.py:16
  1228.1 126.1 %while.59 = (s32[]{:T(128)}, f32[6,256,2,64]{1,3,2,0:T(8,128)}, f32[6,3328,2,64]{1,3,2,0:T(8,128)}, f32[6,3328,2,64]{1,3,2,0:T(8,128)}, bf16[6,3328,2,64]{1,3,2,...) while((s32[]{:T(128)}, f32[6,256,2,64]{1,3,2,0:T(8,128)}, ...), condition=%wide.region_27.28_spmd.clone, body=%wide.region_25.27_spmd.clone.sunk | while | flops 1107557888 | bytes 75987424 | solution.py:257
  1354.3 16.8 fusion.90
  1376.7 9.0 collective-permute-start.49
  1387.0 22.9 collective-permute-start.51
  1411.3 12.6 collective-permute-start.53
  1425.2 65.7 %collective-permute-done.50 = bf16[256,1536]{0,1:T(8,128)(2,1)S(1)} collective-permute-done((bf16[256,1536]{0,1:T(8,128)(2,1)S(1)}, bf16[256,1536]{0,1:T(8,128)(2,1)S(1)}, u32[]{:S(2)}, u32[]{:S(2)}) %collective-permute-start.50) | collective-permute-done | bytes 786464 | tf_op jit(solution)/shard_map/ppermute | solution.py:16
  1499.8 15.8 collective-permute-start.57
  1517.0 49.1 %collective-permute-start.59 = (bf16[256,1536]{0,1:T(8,128)(2,1)S(1)}, bf16[256,1536]{0,1:T(8,128)(2,1)S(1)}, u32[]{:S(2)}, u32[]{:S(2)}) collective-permute-start(bf16[256,1536]{0,1:T(8,128)(2,1)S(1)} %get-tuple-element.516), channel_id=1, source_target_pairs={{0,6},{1,7},{2,8},{3,9},{4,10},{5,11},{6,12},{7,13},{8,14},{9,15},... | collective-permute-start | bytes 2359304 | tf_op jit(solution)/shard_map/ppermute | solution.py:16
  1567.6 20.7 collective-permute-done.58
  1641.3 78.9 %reduce-scatter.27.cloned.1.call-done = bf16[96,2304]{1,0:T(8,128)(2,1)} async-done(((bf16[768,2304]{1,0:T(8,128)(2,1)}), bf16[96,2304]{1,0:T(8,128)(2,1)}) %reduce-scatter.27.cloned.1.call-update) | async-done | bytes 442384 | tf_op jit(solution)/shard_map/reduce_scatter | solution.py:307
  1720.3 39.9 %reduce-scatter.33.cloned.1.call-done = bf16[96,768]{1,0:T(8,128)(2,1)} async-done(((bf16[768,768]{1,0:T(8,128)(2,1)}), bf16[96,768]{1,0:T(8,128)(2,1)}) %reduce-scatter.33.cloned.1.call-update) | async-done | bytes 147472 | tf_op jit(solution)/shard_map/reduce_scatter | solution.py:313
  1760.2 39.8 %reduce-scatter.31.cloned.1.call-done = bf16[96,768]{1,0:T(8,128)(2,1)} async-done(((bf16[768,768]{1,0:T(8,128)(2,1)}), bf16[96,768]{1,0:T(8,128)(2,1)}) %reduce-scatter.31.cloned.1.call-update) | async-done | bytes 147472 | tf_op jit(solution)/shard_map/reduce_scatter | solution.py:313
  1800.0 57.2 %reduce-scatter.37.cloned.1.call-done = bf16[96,3072]{1,0:T(8,128)(2,1)} async-done(((bf16[768,3072]{1,0:T(8,128)(2,1)}), bf16[96,3072]{1,0:T(8,128)(2,1)}) %reduce-scatter.37.cloned.1.call-update) | async-done | bytes 589840 | tf_op jit(solution)/shard_map/reduce_scatter | solution.py:316
  1857.2 57.1 %reduce-scatter.41.cloned.1.call-done = bf16[384,768]{1,0:T(8,128)(2,1)} async-done(((bf16[3072,768]{1,0:T(8,128)(2,1)}), bf16[384,768]{1,0:T(8,128)(2,1)}) %reduce-scatter.41.cloned.1.call-update) | async-done | bytes 589840 | tf_op jit(solution)/shard_map/reduce_scatter | solution.py:322
  1914.3 57.1 %reduce-scatter.39.cloned.1.call-done = bf16[384,768]{1,0:T(8,128)(2,1)} async-done(((bf16[3072,768]{1,0:T(8,128)(2,1)}), bf16[384,768]{1,0:T(8,128)(2,1)}) %reduce-scatter.39.cloned.1.call-update) | async-done | bytes 589840 | tf_op jit(solution)/shard_map/reduce_scatter | solution.py:322
  1971.4 57.1 %reduce-scatter.35.cloned.1.call-done = bf16[96,3072]{1,0:T(8,128)(2,1)} async-done(((bf16[768,3072]{1,0:T(8,128)(2,1)}), bf16[96,3072]{1,0:T(8,128)(2,1)}) %reduce-scatter.35.cloned.1.call-update) | async-done | bytes 589840 | tf_op jit(solution)/shard_map/reduce_scatter | solution.py:316
  2030.3 22.9 all-reduce.6
  2065.9 36.3 %reduce-scatter.49.cloned.1.call-done = bf16[96,2]{1,0:T(8,128)(2,1)} async-done(((bf16[768,2]{1,0:T(8,128)(2,1)}), bf16[96,2]{1,0:T(8,128)(2,1)}) %reduce-scatter.49.cloned.1.call-update) | async-done | bytes 400
  2103.1 36.5 %reduce-scatter.45.cloned.1.call-done = bf16[96,3]{1,0:T(8,128)(2,1)} async-done(((bf16[768,3]{1,0:T(8,128)(2,1)}), bf16[96,3]{1,0:T(8,128)(2,1)}) %reduce-scatter.45.cloned.1.call-update) | async-done | bytes 592
  2141.6 34.5 %reduce-scatter.51.cloned.1.call-done = bf16[96,2]{1,0:T(8,128)(2,1)} async-done(((bf16[768,2]{1,0:T(8,128)(2,1)}), bf16[96,2]{1,0:T(8,128)(2,1)}) %reduce-scatter.51.cloned.1.call-update) | async-done | bytes 400
  2176.9 35.9 %reduce-scatter.47.cloned.1.call-done = bf16[96,2]{1,0:T(8,128)(2,1)} async-done(((bf16[768,2]{1,0:T(8,128)(2,1)}), bf16[96,2]{1,0:T(8,128)(2,1)}) %reduce-scatter.47.cloned.1.call-update) | async-done | bytes 400
  2213.6 36.4 %reduce-scatter.43.cloned.1.call-done = bf16[96,3]{1,0:T(8,128)(2,1)} async-done(((bf16[768,3]{1,0:T(8,128)(2,1)}), bf16[96,3]{1,0:T(8,128)(2,1)}) %reduce-scatter.43.cloned.1.call-update) | async-done | bytes 592
  2250.9 11.9 all-reduce.7
  2265.7 26.2 %all-gather.49.cloned.1.call-done = bf16[384,2304]{1,0:T(8,128)(2,1)} async-done(((bf16[96,2304]{1,0:T(8,128)(2,1)}), bf16[384,2304]{1,0:T(8,128)(2,1)}) %all-gather.49.cloned.1.call-update) | async-done | bytes 1769488 | tf_op jit(solution)/shard_map/all_gather | solution.py:336
  2293.7 38.8 %all-gather.47.cloned.1.call-done = bf16[384,2304]{1,0:T(8,128)(2,1)} async-done(((bf16[96,2304]{1,0:T(8,128)(2,1)}), bf16[384,2304]{1,0:T(8,128)(2,1)}) %all-gather.47.cloned.1.call-update) | async-done | bytes 1769488 | tf_op jit(solution)/shard_map/all_gather | solution.py:336
  2335.6 103.9 %all-reduce.11.cloned.1.call-done = (bf16[1,96,768]{2,1,0:T(8,128)(2,1)}, bf16[1,96,768]{2,1,0:T(8,128)(2,1)}, bf16[1,96,3072]{2,1,0:T(8,128)(2,1)}, bf16[1,96,3...) async-done(((bf16[1,96,768]{2,1,0:T(8,128)(2,1)}, bf16[1,96,768]{2,1,0:T(8,128)(2,1)}, bf16[1,96,3072]{2,1,0:T(8,128)(2,1)}, ...) | async-done | bytes 2654224 | tf_op jit(solution)/shard_map/psum | solution.py:338
  (800 shorter events, 713.3 us)
Async XLA Ops:
  7.2 155.8 %all-gather.31.cloned.1.call-start = ((), (), s32[]{:S(2)}) async-start(), calls=%async_computation.22 | async-start | bytes 3981312 | tf_op jit(solution)/shard_map/all_gather | solution.py:100
  9.5 457.6 %all-gather.33.cloned.1.call-start = ((), (), s32[]{:S(2)}) async-start(), calls=%async_computation.23 | async-start | bytes 1327104 | tf_op jit(solution)/shard_map/all_gather | solution.py:102
  11.3 458.2 %all-gather.35.cloned.1.call-start = ((), (), s32[]{:S(2)}) async-start(), calls=%async_computation.24 | async-start | bytes 5308416 | tf_op jit(solution)/shard_map/all_gather | solution.py:103
  12.5 468.5 %all-gather.37.cloned.1.call-start = ((), (), s32[]{:S(2)}) async-start(), calls=%async_computation.25 | async-start | bytes 5308416 | tf_op jit(solution)/shard_map/all_gather | solution.py:105
  13.7 472.0 %all-gather.39.cloned.1.call-start = ((), (), s32[]{:S(2)}) async-start(), calls=%async_computation.26 | async-start | bytes 3981312 | tf_op jit(solution)/shard_map/all_gather | solution.py:100
  14.3 784.8 %all-gather.41.cloned.1.call-start = ((), (), s32[]{:S(2)}) async-start(), calls=%async_computation.27 | async-start | bytes 1327104 | tf_op jit(solution)/shard_map/all_gather | solution.py:102
  14.9 786.5 %all-gather.43.cloned.1.call-start = ((), (), s32[]{:S(2)}) async-start(), calls=%async_computation.28 | async-start | bytes 5308416 | tf_op jit(solution)/shard_map/all_gather | solution.py:103
  14.9 139.6 %collective-permute-start.12 = (s32[256]{0:T(256)S(1)}, s32[256]{0:T(256)S(1)}, u32[]{:S(2)}, u32[]{:S(2)}) collective-permute-start(s32[256]{0:T(256)S(1)} %broadcast_add_fusion), channel_id=1, source_target_pairs={{0,6},{1,7},{2,8},{3,9},{4,10},{5,11},{6,12},{7,13},{8,14},{9,15},... | collective-permute-start | bytes 3080 | tf_op jit(solution)/shard_map/ppermute | solution.py:16
  20.4 137.1 %collective-permute-start.13 = (s32[256]{0:T(256)S(1)}, s32[256]{0:T(256)S(1)}, u32[]{:S(2)}, u32[]{:S(2)}) collective-permute-start(s32[256]{0:T(256)S(1)} %broadcast_add_fusion), channel_id=1, source_target_pairs={{0,5},{1,6},{2,7},{3,8},{4,9},{5,10},{6,11},{7,12},{8,13},{9,14},{... | collective-permute-start | bytes 3080 | tf_op jit(solution)/shard_map/ppermute | solution.py:16
  25.1 133.7 %collective-permute-start.14 = (s32[256]{0:T(256)S(1)}, s32[256]{0:T(256)S(1)}, u32[]{:S(2)}, u32[]{:S(2)}) collective-permute-start(s32[256]{0:T(256)S(1)} %broadcast_add_fusion), channel_id=1, source_target_pairs={{0,4},{1,5},{2,6},{3,7},{4,8},{5,9},{6,10},{7,11},{8,12},{9,13},{1... | collective-permute-start | bytes 3080 | tf_op jit(solution)/shard_map/ppermute | solution.py:16
  26.8 133.3 %collective-permute-start.15 = (s32[256]{0:T(256)S(1)}, s32[256]{0:T(256)S(1)}, u32[]{:S(2)}, u32[]{:S(2)}) collective-permute-start(s32[256]{0:T(256)S(1)} %broadcast_add_fusion), channel_id=1, source_target_pairs={{0,3},{1,4},{2,5},{3,6},{4,7},{5,8},{6,9},{7,10},{8,11},{9,12},{10... | collective-permute-start | bytes 3080 | tf_op jit(solution)/shard_map/ppermute | solution.py:16
  32.2 129.3 %collective-permute-start.16 = (s32[256]{0:T(256)S(1)}, s32[256]{0:T(256)S(1)}, u32[]{:S(2)}, u32[]{:S(2)}) collective-permute-start(s32[256]{0:T(256)S(1)} %broadcast_add_fusion), channel_id=1, source_target_pairs={{0,2},{1,3},{2,4},{3,5},{4,6},{5,7},{6,8},{7,9},{8,10},{9,11},{10,... | collective-permute-start | bytes 3080 | tf_op jit(solution)/shard_map/ppermute | solution.py:16
  33.5 779.0 %all-gather.45.cloned.1.call-start = ((), (), s32[]{:S(2)}) async-start(), calls=%async_computation.29 | async-start | bytes 5308416 | tf_op jit(solution)/shard_map/all_gather | solution.py:105
  166.4 72.1 %collective-permute-start = (bf16[256,1536]{1,0:T(8,128)(2,1)S(1)}, bf16[256,1536]{1,0:T(8,128)(2,1)}, u32[]{:S(2)}, u32[]{:S(2)}) collective-permute-start(bf16[256,1536]{1,0:T(8,128)(2,1)S(1)} %pad_maximum_fusion.4), channel_id=1, source_target_pairs={{0,6},{1,7},{2,8},{3,9},{4,10},{5,11},{6,12},{7,13},{8,14},{9,15},... | collective-permute-start | bytes 2359304 | tf_op jit(solution)/shard_map/ppermute | solution.py:16
  178.3 95.2 %collective-permute-start.1 = (bf16[256,1536]{1,0:T(8,128)(2,1)S(1)}, bf16[256,1536]{1,0:T(8,128)(2,1)}, u32[]{:S(2)}, u32[]{:S(2)}) collective-permute-start(bf16[256,1536]{1,0:T(8,128)(2,1)S(1)} %pad_maximum_fusion.4), channel_id=1, source_target_pairs={{0,5},{1,6},{2,7},{3,8},{4,9},{5,10},{6,11},{7,12},{8,13},{9,14},{... | collective-permute-start | bytes 2359304 | tf_op jit(solution)/shard_map/ppermute | solution.py:16
  186.7 90.0 %collective-permute-start.2 = (bf16[256,1536]{1,0:T(8,128)(2,1)S(1)}, bf16[256,1536]{1,0:T(8,128)(2,1)}, u32[]{:S(2)}, u32[]{:S(2)}) collective-permute-start(bf16[256,1536]{1,0:T(8,128)(2,1)S(1)} %pad_maximum_fusion.4), channel_id=1, source_target_pairs={{0,4},{1,5},{2,6},{3,7},{4,8},{5,9},{6,10},{7,11},{8,12},{9,13},{1... | collective-permute-start | bytes 2359304 | tf_op jit(solution)/shard_map/ppermute | solution.py:16
  190.0 90.1 %collective-permute-start.3 = (bf16[256,1536]{1,0:T(8,128)(2,1)S(1)}, bf16[256,1536]{1,0:T(8,128)(2,1)}, u32[]{:S(2)}, u32[]{:S(2)}) collective-permute-start(bf16[256,1536]{1,0:T(8,128)(2,1)S(1)} %pad_maximum_fusion.4), channel_id=1, source_target_pairs={{0,3},{1,4},{2,5},{3,6},{4,7},{5,8},{6,9},{7,10},{8,11},{9,12},{10... | collective-permute-start | bytes 2359304 | tf_op jit(solution)/shard_map/ppermute | solution.py:16
  276.8 102.7 %collective-permute-start.7 = (bf16[256,1536]{1,0:T(8,128)(2,1)S(1)}, bf16[256,1536]{1,0:T(8,128)(2,1)S(1)}, u32[]{:S(2)}, u32[]{:S(2)}) collective-permute-start(bf16[256,1536]{1,0:T(8,128)(2,1)S(1)} %pad_maximum_fusion.4), channel_id=1, source_target_pairs={{2,0},{3,1},{4,2},{5,3},{6,4},{7,5},{8,6},{9,7},{10,8},{11,9},{12,... | collective-permute-start | bytes 2359304 | tf_op jit(solution)/shard_map/ppermute | solution.py:16
  280.1 100.4 %collective-permute-start.8 = (bf16[256,1536]{1,0:T(8,128)(2,1)S(1)}, bf16[256,1536]{1,0:T(8,128)(2,1)S(1)}, u32[]{:S(2)}, u32[]{:S(2)}) collective-permute-start(bf16[256,1536]{1,0:T(8,128)(2,1)S(1)} %pad_maximum_fusion.4), channel_id=1, source_target_pairs={{3,0},{4,1},{5,2},{6,3},{7,4},{8,5},{9,6},{10,7},{11,8},{12,9},{13... | collective-permute-start | bytes 2359304 | tf_op jit(solution)/shard_map/ppermute | solution.py:16
  283.5 98.0 %collective-permute-start.9 = (bf16[256,1536]{1,0:T(8,128)(2,1)S(1)}, bf16[256,1536]{1,0:T(8,128)(2,1)S(1)}, u32[]{:S(2)}, u32[]{:S(2)}) collective-permute-start(bf16[256,1536]{1,0:T(8,128)(2,1)S(1)} %pad_maximum_fusion.4), channel_id=1, source_target_pairs={{4,0},{5,1},{6,2},{7,3},{8,4},{9,5},{10,6},{11,7},{12,8},{13,9},{1... | collective-permute-start | bytes 2359304 | tf_op jit(solution)/shard_map/ppermute | solution.py:16
  289.2 93.2 %collective-permute-start.10 = (bf16[256,1536]{1,0:T(8,128)(2,1)S(1)}, bf16[256,1536]{1,0:T(8,128)(2,1)S(1)}, u32[]{:S(2)}, u32[]{:S(2)}) collective-permute-start(bf16[256,1536]{1,0:T(8,128)(2,1)S(1)} %pad_maximum_fusion.4), channel_id=1, source_target_pairs={{5,0},{6,1},{7,2},{8,3},{9,4},{10,5},{11,6},{12,7},{13,8},{14,9},{... | collective-permute-start | bytes 2359304 | tf_op jit(solution)/shard_map/ppermute | solution.py:16
  310.9 85.0 %collective-permute-start.11 = (bf16[256,1536]{1,0:T(8,128)(2,1)S(1)}, bf16[256,1536]{1,0:T(8,128)(2,1)S(1)}, u32[]{:S(2)}, u32[]{:S(2)}) collective-permute-start(bf16[256,1536]{1,0:T(8,128)(2,1)S(1)} %pad_maximum_fusion.4), channel_id=1, source_target_pairs={{6,0},{7,1},{8,2},{9,3},{10,4},{11,5},{12,6},{13,7},{14,8},{15,9},... | collective-permute-start | bytes 2359304 | tf_op jit(solution)/shard_map/ppermute | solution.py:16
  489.6 92.3 %collective-permute-start.24 = (bf16[256,1536]{1,0:T(8,128)(2,1)S(1)}, bf16[256,1536]{1,0:T(8,128)(2,1)}, u32[]{:S(2)}, u32[]{:S(2)}) collective-permute-start(bf16[256,1536]{1,0:T(8,128)(2,1)S(1)} %pad_maximum_fusion.5), channel_id=1, source_target_pairs={{0,6},{1,7},{2,8},{3,9},{4,10},{5,11},{6,12},{7,13},{8,14},{9,15},... | collective-permute-start | bytes 2359304 | tf_op jit(solution)/shard_map/ppermute | solution.py:16
  507.0 78.3 %collective-permute-start.25 = (bf16[256,1536]{1,0:T(8,128)(2,1)S(1)}, bf16[256,1536]{1,0:T(8,128)(2,1)}, u32[]{:S(2)}, u32[]{:S(2)}) collective-permute-start(bf16[256,1536]{1,0:T(8,128)(2,1)S(1)} %pad_maximum_fusion.5), channel_id=1, source_target_pairs={{0,5},{1,6},{2,7},{3,8},{4,9},{5,10},{6,11},{7,12},{8,13},{9,14},{... | collective-permute-start | bytes 2359304 | tf_op jit(solution)/shard_map/ppermute | solution.py:16
  523.8 68.3 %collective-permute-start.27 = (bf16[256,1536]{1,0:T(8,128)(2,1)S(1)}, bf16[256,1536]{1,0:T(8,128)(2,1)}, u32[]{:S(2)}, u32[]{:S(2)}) collective-permute-start(bf16[256,1536]{1,0:T(8,128)(2,1)S(1)} %pad_maximum_fusion.5), channel_id=1, source_target_pairs={{0,3},{1,4},{2,5},{3,6},{4,7},{5,8},{6,9},{7,10},{8,11},{9,12},{10... | collective-permute-start | bytes 2359304 | tf_op jit(solution)/shard_map/ppermute | solution.py:16
  529.4 1111.1 %reduce-scatter.29.cloned.1.call-start = ((), (), s32[]{:S(2)}) async-start(), calls=%async_computation.15 | async-start | bytes 3981312 | tf_op jit(solution)/shard_map/reduce_scatter | solution.py:307
  588.7 125.5 %collective-permute-start.31 = (bf16[256,1536]{1,0:T(8,128)(2,1)S(1)}, bf16[256,1536]{1,0:T(8,128)(2,1)S(1)}, u32[]{:S(2)}, u32[]{:S(2)}) collective-permute-start(bf16[256,1536]{1,0:T(8,128)(2,1)S(1)} %pad_maximum_fusion.5), channel_id=1, source_target_pairs={{2,0},{3,1},{4,2},{5,3},{6,4},{7,5},{8,6},{9,7},{10,8},{11,9},{12,... | collective-permute-start | bytes 2359304 | tf_op jit(solution)/shard_map/ppermute | solution.py:16
  592.1 123.2 %collective-permute-start.32 = (bf16[256,1536]{1,0:T(8,128)(2,1)S(1)}, bf16[256,1536]{1,0:T(8,128)(2,1)S(1)}, u32[]{:S(2)}, u32[]{:S(2)}) collective-permute-start(bf16[256,1536]{1,0:T(8,128)(2,1)S(1)} %pad_maximum_fusion.5), channel_id=1, source_target_pairs={{3,0},{4,1},{5,2},{6,3},{7,4},{8,5},{9,6},{10,7},{11,8},{12,9},{13... | collective-permute-start | bytes 2359304 | tf_op jit(solution)/shard_map/ppermute | solution.py:16
  598.7 117.5 %collective-permute-start.33 = (bf16[256,1536]{1,0:T(8,128)(2,1)S(1)}, bf16[256,1536]{1,0:T(8,128)(2,1)S(1)}, u32[]{:S(2)}, u32[]{:S(2)}) collective-permute-start(bf16[256,1536]{1,0:T(8,128)(2,1)S(1)} %pad_maximum_fusion.5), channel_id=1, source_target_pairs={{4,0},{5,1},{6,2},{7,3},{8,4},{9,5},{10,6},{11,7},{12,8},{13,9},{1... | collective-permute-start | bytes 2359304 | tf_op jit(solution)/shard_map/ppermute | solution.py:16
  615.6 101.6 %collective-permute-start.34 = (bf16[256,1536]{1,0:T(8,128)(2,1)S(1)}, bf16[256,1536]{1,0:T(8,128)(2,1)S(1)}, u32[]{:S(2)}, u32[]{:S(2)}) collective-permute-start(bf16[256,1536]{1,0:T(8,128)(2,1)S(1)} %pad_maximum_fusion.5), channel_id=1, source_target_pairs={{5,0},{6,1},{7,2},{8,3},{9,4},{10,5},{11,6},{12,7},{13,8},{14,9},{... | collective-permute-start | bytes 2359304 | tf_op jit(solution)/shard_map/ppermute | solution.py:16
  627.6 100.3 %collective-permute-start.35 = (bf16[256,1536]{1,0:T(8,128)(2,1)S(1)}, bf16[256,1536]{1,0:T(8,128)(2,1)S(1)}, u32[]{:S(2)}, u32[]{:S(2)}) collective-permute-start(bf16[256,1536]{1,0:T(8,128)(2,1)S(1)} %pad_maximum_fusion.5), channel_id=1, source_target_pairs={{6,0},{7,1},{8,2},{9,3},{10,4},{11,5},{12,6},{13,7},{14,8},{15,9},... | collective-permute-start | bytes 2359304 | tf_op jit(solution)/shard_map/ppermute | solution.py:16
  980.0 110.3 %collective-permute-start.38 = (bf16[256,1536]{0,1:T(8,128)(2,1)S(1)}, bf16[256,1536]{0,1:T(8,128)(2,1)S(1)}, u32[]{:S(2)}, u32[]{:S(2)}) collective-permute-start(bf16[256,1536]{0,1:T(8,128)(2,1)S(1)} %get-tuple-element.537), channel_id=1, source_target_pairs={{2,0},{3,1},{4,2},{5,3},{6,4},{7,5},{8,6},{9,7},{10,8},{11,9},{12,... | collective-permute-start | bytes 2359304 | tf_op jit(solution)/shard_map/ppermute | solution.py:16
  981.3 115.5 %collective-permute-start.39 = (bf16[256,1536]{0,1:T(8,128)(2,1)S(1)}, bf16[256,1536]{0,1:T(8,128)(2,1)S(1)}, u32[]{:S(2)}, u32[]{:S(2)}) collective-permute-start(bf16[256,1536]{0,1:T(8,128)(2,1)S(1)} %get-tuple-element.536), channel_id=1, source_target_pairs={{0,2},{1,3},{2,4},{3,5},{4,6},{5,7},{6,8},{7,9},{8,10},{9,11},{10,... | collective-permute-start | bytes 2359304 | tf_op jit(solution)/shard_map/ppermute | solution.py:16
  1008.8 89.3 %collective-permute-start.40 = (bf16[256,1536]{0,1:T(8,128)(2,1)S(1)}, bf16[256,1536]{0,1:T(8,128)(2,1)S(1)}, u32[]{:S(2)}, u32[]{:S(2)}) collective-permute-start(bf16[256,1536]{0,1:T(8,128)(2,1)S(1)} %get-tuple-element.535), channel_id=1, source_target_pairs={{3,0},{4,1},{5,2},{6,3},{7,4},{8,5},{9,6},{10,7},{11,8},{12,9},{13... | collective-permute-start | bytes 2359304 | tf_op jit(solution)/shard_map/ppermute | solution.py:16
  1010.1 95.0 %collective-permute-start.41 = (bf16[256,1536]{0,1:T(8,128)(2,1)S(1)}, bf16[256,1536]{0,1:T(8,128)(2,1)S(1)}, u32[]{:S(2)}, u32[]{:S(2)}) collective-permute-start(bf16[256,1536]{0,1:T(8,128)(2,1)S(1)} %get-tuple-element.534), channel_id=1, source_target_pairs={{0,3},{1,4},{2,5},{3,6},{4,7},{5,8},{6,9},{7,10},{8,11},{9,12},{10... | collective-permute-start | bytes 2359304 | tf_op jit(solution)/shard_map/ppermute | solution.py:16
  1022.3 84.1 %collective-permute-start.42 = (bf16[256,1536]{0,1:T(8,128)(2,1)S(1)}, bf16[256,1536]{0,1:T(8,128)(2,1)S(1)}, u32[]{:S(2)}, u32[]{:S(2)}) collective-permute-start(bf16[256,1536]{0,1:T(8,128)(2,1)S(1)} %get-tuple-element.533), channel_id=1, source_target_pairs={{4,0},{5,1},{6,2},{7,3},{8,4},{9,5},{10,6},{11,7},{12,8},{13,9},{1... | collective-permute-start | bytes 2359304 | tf_op jit(solution)/shard_map/ppermute | solution.py:16
  1105.1 89.5 %collective-permute-start.46 = (bf16[256,1536]{0,1:T(8,128)(2,1)S(1)}, bf16[256,1536]{0,1:T(8,128)(2,1)S(1)}, u32[]{:S(2)}, u32[]{:S(2)}) collective-permute-start(bf16[256,1536]{0,1:T(8,128)(2,1)S(1)} %get-tuple-element.529), channel_id=1, source_target_pairs={{6,0},{7,1},{8,2},{9,3},{10,4},{11,5},{12,6},{13,7},{14,8},{15,9},... | collective-permute-start | bytes 2359304 | tf_op jit(solution)/shard_map/ppermute | solution.py:16
  1106.4 88.2 %collective-permute-start.47 = (bf16[256,1536]{0,1:T(8,128)(2,1)S(1)}, bf16[256,1536]{0,1:T(8,128)(2,1)S(1)}, u32[]{:S(2)}, u32[]{:S(2)}) collective-permute-start(bf16[256,1536]{0,1:T(8,128)(2,1)S(1)} %get-tuple-element.528), channel_id=1, source_target_pairs={{0,6},{1,7},{2,8},{3,9},{4,10},{5,11},{6,12},{7,13},{8,14},{9,15},... | collective-permute-start | bytes 2359304 | tf_op jit(solution)/shard_map/ppermute | solution.py:16
  1354.2 366.0 %reduce-scatter.27.cloned.1.call-start = ((), (), s32[]{:S(2)}) async-start(), calls=%async_computation.14 | async-start | bytes 3981312 | tf_op jit(solution)/shard_map/reduce_scatter | solution.py:307
  1385.7 105.2 %collective-permute-start.50 = (bf16[256,1536]{0,1:T(8,128)(2,1)S(1)}, bf16[256,1536]{0,1:T(8,128)(2,1)S(1)}, u32[]{:S(2)}, u32[]{:S(2)}) collective-permute-start(bf16[256,1536]{0,1:T(8,128)(2,1)S(1)} %get-tuple-element.525), channel_id=1, source_target_pairs={{2,0},{3,1},{4,2},{5,3},{6,4},{7,5},{8,6},{9,7},{10,8},{11,9},{12,... | collective-permute-start | bytes 2359304 | tf_op jit(solution)/shard_map/ppermute | solution.py:16
  1387.0 111.5 %collective-permute-start.51 = (bf16[256,1536]{0,1:T(8,128)(2,1)S(1)}, bf16[256,1536]{0,1:T(8,128)(2,1)S(1)}, u32[]{:S(2)}, u32[]{:S(2)}) collective-permute-start(bf16[256,1536]{0,1:T(8,128)(2,1)S(1)} %get-tuple-element.524), channel_id=1, source_target_pairs={{0,2},{1,3},{2,4},{3,5},{4,6},{5,7},{6,8},{7,9},{8,10},{9,11},{10,... | collective-permute-start | bytes 2359304 | tf_op jit(solution)/shard_map/ppermute | solution.py:16
  1410.0 89.9 %collective-permute-start.52 = (bf16[256,1536]{0,1:T(8,128)(2,1)S(1)}, bf16[256,1536]{0,1:T(8,128)(2,1)S(1)}, u32[]{:S(2)}, u32[]{:S(2)}) collective-permute-start(bf16[256,1536]{0,1:T(8,128)(2,1)S(1)} %get-tuple-element.523), channel_id=1, source_target_pairs={{3,0},{4,1},{5,2},{6,3},{7,4},{8,5},{9,6},{10,7},{11,8},{12,9},{13... | collective-permute-start | bytes 2359304 | tf_op jit(solution)/shard_map/ppermute | solution.py:16
  1411.3 104.4 %collective-permute-start.53 = (bf16[256,1536]{0,1:T(8,128)(2,1)S(1)}, bf16[256,1536]{0,1:T(8,128)(2,1)S(1)}, u32[]{:S(2)}, u32[]{:S(2)}) collective-permute-start(bf16[256,1536]{0,1:T(8,128)(2,1)S(1)} %get-tuple-element.522), channel_id=1, source_target_pairs={{0,3},{1,4},{2,5},{3,6},{4,7},{5,8},{6,9},{7,10},{8,11},{9,12},{10... | collective-permute-start | bytes 2359304 | tf_op jit(solution)/shard_map/ppermute | solution.py:16
  1423.9 93.1 %collective-permute-start.54 = (bf16[256,1536]{0,1:T(8,128)(2,1)S(1)}, bf16[256,1536]{0,1:T(8,128)(2,1)S(1)}, u32[]{:S(2)}, u32[]{:S(2)}) collective-permute-start(bf16[256,1536]{0,1:T(8,128)(2,1)S(1)} %get-tuple-element.521), channel_id=1, source_target_pairs={{4,0},{5,1},{6,2},{7,3},{8,4},{9,5},{10,6},{11,7},{12,8},{13,9},{1... | collective-permute-start | bytes 2359304 | tf_op jit(solution)/shard_map/ppermute | solution.py:16
  1490.9 76.6 %collective-permute-start.55 = (bf16[256,1536]{0,1:T(8,128)(2,1)S(1)}, bf16[256,1536]{0,1:T(8,128)(2,1)S(1)}, u32[]{:S(2)}, u32[]{:S(2)}) collective-permute-start(bf16[256,1536]{0,1:T(8,128)(2,1)S(1)} %get-tuple-element.520), channel_id=1, source_target_pairs={{0,4},{1,5},{2,6},{3,7},{4,8},{5,9},{6,10},{7,11},{8,12},{9,13},{1... | collective-permute-start | bytes 2359304 | tf_op jit(solution)/shard_map/ppermute | solution.py:16
  1498.5 69.0 %collective-permute-start.56 = (bf16[256,1536]{0,1:T(8,128)(2,1)S(1)}, bf16[256,1536]{0,1:T(8,128)(2,1)S(1)}, u32[]{:S(2)}, u32[]{:S(2)}) collective-permute-start(bf16[256,1536]{0,1:T(8,128)(2,1)S(1)} %get-tuple-element.519), channel_id=1, source_target_pairs={{5,0},{6,1},{7,2},{8,3},{9,4},{10,5},{11,6},{12,7},{13,8},{14,9},{... | collective-permute-start | bytes 2359304 | tf_op jit(solution)/shard_map/ppermute | solution.py:16
  1499.8 67.7 %collective-permute-start.57 = (bf16[256,1536]{0,1:T(8,128)(2,1)S(1)}, bf16[256,1536]{0,1:T(8,128)(2,1)S(1)}, u32[]{:S(2)}, u32[]{:S(2)}) collective-permute-start(bf16[256,1536]{0,1:T(8,128)(2,1)S(1)} %get-tuple-element.518), channel_id=1, source_target_pairs={{0,5},{1,6},{2,7},{3,8},{4,9},{5,10},{6,11},{7,12},{8,13},{9,14},{... | collective-permute-start | bytes 2359304 | tf_op jit(solution)/shard_map/ppermute | solution.py:16
  1515.7 72.6 %collective-permute-start.58 = (bf16[256,1536]{0,1:T(8,128)(2,1)S(1)}, bf16[256,1536]{0,1:T(8,128)(2,1)S(1)}, u32[]{:S(2)}, u32[]{:S(2)}) collective-permute-start(bf16[256,1536]{0,1:T(8,128)(2,1)S(1)} %get-tuple-element.517), channel_id=1, source_target_pairs={{6,0},{7,1},{8,2},{9,3},{10,4},{11,5},{12,6},{13,7},{14,8},{15,9},... | collective-permute-start | bytes 2359304 | tf_op jit(solution)/shard_map/ppermute | solution.py:16
  1517.0 72.2 %collective-permute-start.59 = (bf16[256,1536]{0,1:T(8,128)(2,1)S(1)}, bf16[256,1536]{0,1:T(8,128)(2,1)S(1)}, u32[]{:S(2)}, u32[]{:S(2)}) collective-permute-start(bf16[256,1536]{0,1:T(8,128)(2,1)S(1)} %get-tuple-element.516), channel_id=1, source_target_pairs={{0,6},{1,7},{2,8},{3,9},{4,10},{5,11},{6,12},{7,13},{8,14},{9,15},... | collective-permute-start | bytes 2359304 | tf_op jit(solution)/shard_map/ppermute | solution.py:16
  1599.4 160.8 %reduce-scatter.33.cloned.1.call-start = ((), (), s32[]{:S(2)}) async-start(), calls=%async_computation.17 | async-start | bytes 1327104 | tf_op jit(solution)/shard_map/reduce_scatter | solution.py:313
  1602.0 198.0 %reduce-scatter.31.cloned.1.call-start = ((), (), s32[]{:S(2)}) async-start(), calls=%async_computation.16 | async-start | bytes 1327104 | tf_op jit(solution)/shard_map/reduce_scatter | solution.py:313
  1604.6 252.6 %reduce-scatter.37.cloned.1.call-start = ((), (), s32[]{:S(2)}) async-start(), calls=%async_computation.19 | async-start | bytes 5308416 | tf_op jit(solution)/shard_map/reduce_scatter | solution.py:316
  1609.9 304.5 %reduce-scatter.41.cloned.1.call-start = ((), (), s32[]{:S(2)}) async-start(), calls=%async_computation.21 | async-start | bytes 5308416 | tf_op jit(solution)/shard_map/reduce_scatter | solution.py:322
  1616.0 355.5 %reduce-scatter.39.cloned.1.call-start = ((), (), s32[]{:S(2)}) async-start(), calls=%async_computation.20 | async-start | bytes 5308416 | tf_op jit(solution)/shard_map/reduce_scatter | solution.py:322
  1622.2 406.4 %reduce-scatter.35.cloned.1.call-start = ((), (), s32[]{:S(2)}) async-start(), calls=%async_computation.18 | async-start | bytes 5308416 | tf_op jit(solution)/shard_map/reduce_scatter | solution.py:316
  1628.0 437.1 %reduce-scatter.53.cloned.1.call-start = ((), (), s32[]{:S(2)}) async-start(), calls=%async_computation.37 | async-start | bytes 221184
  1630.9 471.3 %reduce-scatter.49.cloned.1.call-start = ((), (), s32[]{:S(2)}) async-start(), calls=%async_computation.35 | async-start | bytes 221184
  1631.9 507.6 %reduce-scatter.45.cloned.1.call-start = ((), (), s32[]{:S(2)}) async-start(), calls=%async_computation.33 | async-start | bytes 221184
  1633.0 543.1 %reduce-scatter.51.cloned.1.call-start = ((), (), s32[]{:S(2)}) async-start(), calls=%async_computation.36 | async-start | bytes 221184
  1638.6 574.2 %reduce-scatter.47.cloned.1.call-start = ((), (), s32[]{:S(2)}) async-start(), calls=%async_computation.34 | async-start | bytes 221184
  1639.5 610.5 %reduce-scatter.43.cloned.1.call-start = ((), (), s32[]{:S(2)}) async-start(), calls=%async_computation.32 | async-start | bytes 221184
  1640.5 651.5 %all-gather.49.cloned.1.call-start = ((), (), s32[]{:S(2)}) async-start(), calls=%async_computation.31 | async-start | bytes 2211840 | tf_op jit(solution)/shard_map/all_gather | solution.py:336
  1641.2 691.3 %all-gather.47.cloned.1.call-start = ((), (), s32[]{:S(2)}) async-start(), calls=%async_computation.30 | async-start | bytes 2211840 | tf_op jit(solution)/shard_map/all_gather | solution.py:336
  1720.2 719.3 %all-reduce.11.cloned.1.call-start = ((), (), s32[]{:S(2)}) async-start(), calls=%async_computation.38 | async-start | bytes 5308416 | tf_op jit(solution)/shard_map/psum | solution.py:338
  (164 other events, 9811.1 us)
Sparse Core Ops, SparseCore 0:
  10.5 38.1 all-gather.30
  50.5 24.4 all-gather.32
  77.5 40.8 all-gather.34
  120.7 38.9 all-gather.36
  162.0 33.7 all-gather.38
  197.6 56.5 all-gather.40
  256.6 47.5 all-gather.42
  529.5 74.4 all-gather.44
  1354.3 99.2 reduce-scatter.28
  1599.4 120.7 reduce-scatter.26
  1723.4 36.6 reduce-scatter.32
  1763.3 36.6 reduce-scatter.30
  1803.4 53.7 reduce-scatter.36
  1860.5 53.7 reduce-scatter.40
  1917.6 53.7 reduce-scatter.38
  1974.7 53.7 reduce-scatter.34
  2031.4 33.6 reduce-scatter.52
  2068.6 33.6 reduce-scatter.48
  2105.9 33.6 reduce-scatter.44
  2142.4 33.6 reduce-scatter.50
  2179.1 33.6 reduce-scatter.46
  2216.4 33.6 reduce-scatter.42
  2251.6 40.2 all-gather.48
  2293.4 39.0 all-gather.46
  2335.3 104.1 all-reduce.10
